TPU v7x, 128 devices: a whole 4x4x4 slice. The times are simulated.
128 devices in a mesh: pol: 4 (over y_hi, core), fsdp: 32 (over y_lo, z, x).
Axes of the slice: x: 4, y: 4 (y_hi: 2, y_lo: 2; y = y_hi * 2 + y_lo), z: 4, core: 2. Of those that a mesh axis runs over, the one named last changes fastest.
Arguments:
- gate_pre: bfloat16 [4, 4096, 20480], P('pol', None, 'fsdp'), may hold values from -6 to 6
- up_pre: bfloat16 [4, 4096, 20480], P('pol', None, 'fsdp'), may hold values from -360 to 360
- lag: bfloat16 [4, 20480, 2304], P('pol', 'fsdp'), may hold values from -6 to 6
- task: bfloat16 [4, 20480, 2304], P('pol', 'fsdp'), may hold values from -30 to 30
- cotangent: bfloat16 [4, 4096, 2304], P('pol', 'fsdp'), may hold values from -6 to 6
- buckets: int32 [4, 4096], P('pol', 'fsdp'), may hold values from 0 to 31
- advantages: float32 [4, 32], P('pol'), may hold values from -4 to 4
Outputs:
- new_lag: bfloat16 [4, 20480, 2304], P('pol', 'fsdp')
- merged: bfloat16 [4, 20480, 2304], P('pol', 'fsdp')
All inputs are finite; a program needn't handle non-finite values.
Results may differ from a plain program's by a relative error of at most 0.017.
Values may be sent and summed in bfloat16 or wider, within the bound.
A program may use at most 128 MiB of HBM per device.

v0:
```python
import math

import jax
import jax.numpy as jnp
from jax import lax
from jax.sharding import PartitionSpec as P

D = 2304
FF = 20480


kl_coef = 0.5
clip_level = 0.15
step_rate = 8.0
ema_rate = 0.1


def from_partner(block, axis, distance):
    count = lax.axis_size(axis)
    route = []
    for low in range(count):
        high = low | 1 << distance
        if high != low and high < count:
            route += [(low, high), (high, low)]
    return lax.ppermute(block, axis, route)


def copy_for_each(array, axis):
    length = lax.axis_size(axis)
    return lax.all_to_all(
        jnp.broadcast_to(array[None], (length, *array.shape)), axis, 0, 0, tiled=True
    )


def taken_together(array, axis):
    return copy_for_each(array, axis).sum(axis=0)


def in_one(arrays, axis):
    ends = [0]
    for a in arrays:
        ends.append(ends[-1] + a.size)
    total = taken_together(jnp.concatenate([a.ravel() for a in arrays]), axis)
    return tuple((total[b:e].reshape(a.shape) for a, b, e in zip(arrays, ends, ends[1:])))


def slerp_weights(first_sq, second_sq, cross_dot):
    norm_first = jnp.sqrt(first_sq)
    norm_second = jnp.sqrt(second_sq)
    blend = norm_second / (norm_first + norm_second)
    cosine = jnp.clip(cross_dot / (norm_first * norm_second), -1.0, 1.0)
    opening = jnp.arccos(cosine)
    sine_val = jnp.sin(opening)
    weight_first = jnp.sin((1.0 - blend) * opening) / sine_val
    weight_second = jnp.sin(blend * opening) / sine_val
    return (weight_first, weight_second)


def clip_factor(grad_sq):
    return jnp.minimum(1.0, clip_level / (jnp.sqrt(grad_sq / (FF * D)) + 1e-06))


def shards(gate_pre, up_pre, lag, task, cotangent, buckets, advantages):
    task_own = task[0]
    lag_own = lag[0]
    pol_index = lax.axis_index("pol")
    is_first = pol_index % 2 == 0
    partner_task = from_partner(task_own, "pol", 0)
    inv_root = 1.0 / math.sqrt(FF)
    hidden = (
        jax.nn.gelu(gate_pre[0].astype(jnp.float32), approximate=True)
        * up_pre[0].astype(jnp.float32)
    ).astype(jnp.bfloat16)
    chosen = (buckets[0][:, None] == jnp.arange(advantages.shape[1])[None, :]).astype(jnp.float32)
    adv_tok = jnp.dot(chosen, advantages[0], precision=lax.Precision.HIGHEST)
    weighted = adv_tok[:, None] * cotangent[0].astype(jnp.float32)
    row_block = hidden
    kl_gap = lax.psum_scatter(
        (jnp.dot(row_block, lag_own, preferred_element_type=jnp.float32) * inv_root).astype(
            jnp.bfloat16
        ),
        "fsdp",
        scatter_dimension=0,
        tiled=True,
    ).astype(jnp.float32)
    signal = (weighted + kl_coef * kl_gap).astype(jnp.bfloat16)
    row_block = hidden
    summed = lax.dot_general(
        row_block,
        lax.all_gather(signal, "fsdp", axis=0, tiled=True),
        (((0,), (0,)), ((), ())),
        preferred_element_type=jnp.float32,
    )
    gradient = (summed * inv_root).astype(jnp.bfloat16)
    grad_float = gradient.astype(jnp.float32)
    task_float = task_own.astype(jnp.float32)
    partner_grad = from_partner(gradient, "pol", 0)
    part_grad_float = partner_grad.astype(jnp.float32)
    part_task_float = partner_task.astype(jnp.float32)
    dot_sums = in_one(
        (
            jnp.sum(grad_float * grad_float),
            jnp.sum(part_grad_float * part_grad_float),
            jnp.sum(grad_float * part_grad_float),
            jnp.sum(task_float * task_float),
            jnp.sum(part_task_float * part_task_float),
            jnp.sum(task_float * part_task_float),
            jnp.sum(task_float * grad_float),
            jnp.sum(task_float * part_grad_float),
            jnp.sum(part_task_float * grad_float),
            jnp.sum(part_task_float * part_grad_float),
        ),
        "fsdp",
    )
    grad_oo, grad_pp, grad_op, task_oo, task_pp, task_op, tgrad_oo, tgrad_op, tgrad_po, tgrad_pp = (
        dot_sums
    )
    factor_own = clip_factor(grad_oo)
    factor_part = clip_factor(grad_pp)
    scale_own = step_rate * factor_own
    scale_part = step_rate * factor_part
    update_own = scale_own * grad_float
    delta_own = task_float - update_own
    delta_part = part_task_float - scale_part * part_grad_float
    own_total = task_oo - 2.0 * scale_own * tgrad_oo + scale_own * scale_own * grad_oo
    part_total = task_pp - 2.0 * scale_part * tgrad_pp + scale_part * scale_part * grad_pp
    cross_dot = (
        task_op - scale_part * tgrad_op - scale_own * tgrad_po + scale_own * scale_part * grad_op
    )
    first_sq = jnp.where(is_first, own_total, part_total)
    second_sq = jnp.where(is_first, part_total, own_total)
    weight_first, weight_second = slerp_weights(first_sq, second_sq, cross_dot)
    weight_own = jnp.where(is_first, weight_first, weight_second)
    weight_part = jnp.where(is_first, weight_second, weight_first)
    merged = (weight_own * delta_own + weight_part * delta_part).astype(jnp.bfloat16)
    new_lag = ((1.0 - ema_rate) * (lag_own.astype(jnp.float32) - update_own)).astype(jnp.bfloat16)
    return (new_lag[None], merged[None])


def solution(mesh):
    return jax.shard_map(
        shards,
        mesh=mesh,
        in_specs=(
            P("pol", None, "fsdp"),
            P("pol", None, "fsdp"),
            P("pol", "fsdp", None),
            P("pol", "fsdp", None),
            P("pol", "fsdp", None),
            P("pol", "fsdp"),
            P("pol", None),
        ),
        out_specs=(P("pol", "fsdp", None), P("pol", "fsdp", None)),
        check_vma=False,
    )
```

profile of v0, /device:TPU:1, one launch (start us, length us, event | category | flops | bytes accessed | tf_op | source)
XLA Modules:
  0.0 545.9 jit_solution(10627194771370479992)
XLA Ops:
  7.2 0.0 copy-start
  7.2 0.0 reduce-scatter.2.cloned.1.call-start
  7.2 25.1 %multiply_convert_fusion = bf16[4096,2304]{1,0:T(8,128)(2,1)} fusion(bf16[1,4096,640]{2,1,0:T(8,128)(2,1)} %param.8, bf16[1,4096,640]{2,1,0:T(8,128)(2,1)} %param.7, bf16[1,640,2304]{2,1,0:T(8,128)(2,1)} %param.9), kind=kOutput, calls=%fused_computation | convolution fusion | flops 12129927168 | bytes 32309248 | tf_op jit(solution)/shard_map/dot_general | solution.py:79
  32.3 0.0 reduce-scatter.2.cloned.1.call-update
  32.3 0.0 all-gather.2.cloned.1.call-start
  32.4 0.0 copy-done
  32.4 0.6 copy-done.6
  33.0 0.2 convolution_bitcast_fusion
  33.2 206.8 %reduce-scatter.2.cloned.1.call-done = bf16[128,2304]{1,0:T(8,128)(2,1)} async-done(((bf16[4096,2304]{1,0:T(8,128)(2,1)}), bf16[128,2304]{1,0:T(8,128)(2,1)}) %reduce-scatter.2.cloned.1.call-update) | async-done | bytes 589840 | tf_op jit(solution)/shard_map/reduce_scatter | solution.py:78
  240.0 0.0 copy-done.5
  240.0 2.1 fusion.51
  242.1 0.0 all-gather.2.cloned.1.call-update
  242.1 0.0 copy-done.2
  242.1 14.8 %collective-permute-start.1 = (bf16[640,2304]{1,0:T(8,128)(2,1)S(1)}, bf16[640,2304]{1,0:T(8,128)(2,1)}, u32[]{:S(2)}, u32[]{:S(2)}) collective-permute-start(bf16[640,2304]{1,0:T(8,128)(2,1)S(1)} %bitcast.88), channel_id=1, source_target_pairs={{0,32},{32,0},{64,96},{96,64},{1,33},{33,1},{65,97},{97,65},{2,34}... | collective-permute-start | bytes 8847368 | tf_op jit(solution)/shard_map/ppermute | solution.py:25
  256.9 209.1 %all-gather.2.cloned.1.call-done = bf16[4096,2304]{1,0:T(8,128)(2,1)} async-done(((bf16[128,2304]{1,0:T(8,128)(2,1)}), bf16[4096,2304]{1,0:T(8,128)(2,1)}) %all-gather.2.cloned.1.call-update) | async-done | bytes 18874384 | tf_op jit(solution)/shard_map/all_gather | solution.py:90
  466.1 24.6 %fusion.44 = bf16[640,2304]{1,0:T(8,128)(2,1)S(1)} fusion(bf16[4096,2304]{1,0:T(8,128)(2,1)} %all-gather.2.cloned.1.call-done, bf16[1,4096,640]{2,1,0:T(8,128)(2,1)} %param.8, bf16[1,4096,640]{2,1,0:T(8,128)(2,1)} %param.7), kind=kOutput, calls=%fused_computation.65 | convolution fusion | flops 12114001920 | bytes 32309248 | tf_op jit(solution)/shard_map/dot_general | solution.py:88
  490.7 0.0 copy-start.3
  490.7 0.9 collective-permute-start
  491.6 0.0 collective-permute-done.1
  491.6 5.0 collective-permute-done
  496.6 7.5 %fusion.32 = (f32[]{:T(128)}, f32[]{:T(128)}, f32[]{:T(128)}, f32[]{:T(128)}, f32[]{:T(128)}, /*index=5*/f32[]{:T(128)}, f32[]{:T(128)}, f32[]{:T(128)}, f32[]{:T(128)}, f32[]{:T(128)}) fusion(bf16[640,2304]{1,0:T(8,128)(2,1)S(1)} %collective-permute-done, bf16[640,2304]{1,0:T(8,128)(2,1)} %collective-permute-done.1, bf16[1,640,2304]{2,1,0:T(8,128)(2,1)S(1)} %copy-done.2, ...), kind=kLoop, calls=%fused_computation.55 | loop fusion | flops 35389436 | bytes 11796520 | tf_op jit(solution)/shard_map/reduce_sum | solution.py:111
  504.1 0.0 copy-done.3
  504.1 0.0 copy-done.4
  504.1 6.3 %concatenate.3 = f32[10]{0:T(128)S(1)} concatenate(f32[1]{0:T(128)} %bitcast.9, f32[1]{0:T(128)} %bitcast.10, f32[1]{0:T(128)} %bitcast.11, f32[1]{0:T(128)} %bitcast.13, f32[1]{0:T(128)} %bitcast.14, f32[1]{0:T(128)} %bitcast.15, f32[1]{0:T(128)} %bitcast.16, f32[1]{0:T(128)} %bitcast.17, f32[1]{0:T(128)} %bitcast.18, f32[1]{0:T(128)} %bitcast.19), dimensions={0} | concatenate | bytes 80 | tf_op jit(solution)/shard_map/concatenate | solution.py:43
  510.4 0.6 broadcast_in_dim.6
  511.0 4.3 all-to-all-start
  515.3 7.1 %all-to-all-done = f32[32,1,10]{2,1,0:T(1,128)S(1)} async-done(((f32[32,1,10]{2,1,0:T(1,128)}), f32[32,1,10]{2,1,0:T(1,128)S(1)}, u32[]{:S(2)}, u32[]{:S(2)}) %all-to-all-start) | async-done | bytes 1312 | tf_op jit(solution)/shard_map/all_to_all | solution.py:30
  522.4 0.1 reduce_sum.109
  522.5 0.7 fusion.62
  531.6 0.0 copy-start.1
  531.6 7.4 %fusion.47 = (bf16[1,640,2304]{2,1,0:T(8,128)(2,1)}, bf16[1,640,2304]{2,1,0:T(8,128)(2,1)}) fusion(bf16[640,2304]{1,0:T(8,128)(2,1)} %copy-done.4, bf16[640,2304]{1,0:T(8,128)(2,1)} %collective-permute-done.1, bf16[640,2304]{1,0:T(8,128)(2,1)} %copy-done.3, f32[]{:T(128)S(6)} %mul.237, f32[]{:T(128)S(6)} %select_n.24, f32[]{:T(128)S(6)} %select_n.23, ...), kind=kLoop, calls=%fused_computation.66 | loop fusion | flops 23592960 | bytes 20643856 | tf_op jit(solution)/shard_map/broadcast_in_dim | solution.py:137
  539.0 0.0 copy-done.1
  (4 shorter events, 0.0 us)
Async XLA Ops:
  7.2 25.2 %copy-start = (f32[1,32]{1,0:T(1,128)S(1)}, f32[1,32]{1,0:T(1,128)}, u32[]{:S(2)}) copy-start(f32[1,32]{1,0:T(1,128)} %param.13) | copy-start | bytes 388
  7.2 232.8 %reduce-scatter.2.cloned.1.call-start = ((), (), s32[]{:S(2)}) async-start(), calls=%async_computation.2 | async-start | bytes 19464192 | tf_op jit(solution)/shard_map/reduce_scatter | solution.py:78
  32.3 0.7 copy-start.6
  32.3 207.7 %copy-start.5 = (bf16[1,128,2304]{2,1,0:T(8,128)(2,1)S(1)}, bf16[1,128,2304]{2,1,0:T(8,128)(2,1)}, u32[]{:S(2)}) copy-start(bf16[1,128,2304]{2,1,0:T(8,128)(2,1)} %param.11) | copy-start | bytes 1769476
  32.3 209.8 %copy-start.2 = (bf16[1,640,2304]{2,1,0:T(8,128)(2,1)S(1)}, bf16[1,640,2304]{2,1,0:T(8,128)(2,1)}, u32[]{:S(2)}) copy-start(bf16[1,640,2304]{2,1,0:T(8,128)(2,1)} %param.10) | copy-start | bytes 8847364
  32.3 433.7 %all-gather.2.cloned.1.call-start = ((), (), s32[]{:S(2)}) async-start(), calls=%async_computation.3 | async-start | bytes 19464192 | tf_op jit(solution)/shard_map/all_gather | solution.py:90
  242.1 249.5 %collective-permute-start.1 = (bf16[640,2304]{1,0:T(8,128)(2,1)S(1)}, bf16[640,2304]{1,0:T(8,128)(2,1)}, u32[]{:S(2)}, u32[]{:S(2)}) collective-permute-start(bf16[640,2304]{1,0:T(8,128)(2,1)S(1)} %bitcast.88), channel_id=1, source_target_pairs={{0,32},{32,0},{64,96},{96,64},{1,33},{33,1},{65,97},{97,65},{2,34}... | collective-permute-start | bytes 8847368 | tf_op jit(solution)/shard_map/ppermute | solution.py:25
  490.7 13.4 %copy-start.3 = (bf16[640,2304]{1,0:T(8,128)(2,1)}, bf16[640,2304]{1,0:T(8,128)(2,1)S(1)}, u32[]{:S(2)}) copy-start(bf16[640,2304]{1,0:T(8,128)(2,1)S(1)} %fusion.44) | copy-start | bytes 8847364
  490.7 5.9 %collective-permute-start = (bf16[640,2304]{1,0:T(8,128)(2,1)S(1)}, bf16[640,2304]{1,0:T(8,128)(2,1)S(1)}, u32[]{:S(2)}, u32[]{:S(2)}) collective-permute-start(bf16[640,2304]{1,0:T(8,128)(2,1)S(1)} %fusion.44), channel_id=1, source_target_pairs={{0,32},{32,0},{64,96},{96,64},{1,33},{33,1},{65,97},{97,65},{2,34}... | collective-permute-start | bytes 8847368 | tf_op jit(solution)/shard_map/ppermute | solution.py:25
  496.6 7.5 %copy-start.4 = (bf16[640,2304]{1,0:T(8,128)(2,1)}, bf16[640,2304]{1,0:T(8,128)(2,1)S(1)}, u32[]{:S(2)}) copy-start(bf16[640,2304]{1,0:T(8,128)(2,1)S(1)} %collective-permute-done) | copy-start | bytes 8847364
  511.0 11.4 %all-to-all-start = ((f32[32,1,10]{2,1,0:T(1,128)}), f32[32,1,10]{2,1,0:T(1,128)S(1)}, u32[]{:S(2)}, u32[]{:S(2)}) async-start(f32[32,1,10]{2,1,0:T(1,128)} %broadcast_in_dim.6), calls=%async_computation.1 | async-start | bytes 32768 | tf_op jit(solution)/shard_map/all_to_all | solution.py:30
  531.6 7.5 %copy-start.1 = (f32[1,32]{1,0:T(1,128)S(1)}, f32[1,32]{1,0:T(1,128)}, u32[]{:S(2)}) copy-start(f32[1,32]{1,0:T(1,128)} %param.13) | copy-start | bytes 388
Sparse Core Ops, SparseCore 0:
  32.5 207.4 reduce-scatter.1
  242.3 223.7 all-gather.1
where the time goes:
time: 547 us; the launch traced here: 546 us
  waiting for transfers between devices  428 us (78%)
  matrix products  49.9 us (9%)
  between operations  22.5 us (4%)
  starting transfers between devices  20 us (4%)
  other arithmetic  17.1 us (3%)
  local copies, waits for them, and re-layouts  8.21 us (2%)
    all_gather x1, waiting for transfers between devices, shards(): lax.all_gather(signal, 'fsdp', axis=0, tiled=True)  209 us
    reduce_scatter x1, waiting for transfers between devices, shards(): lax.psum_scatter((jnp.dot(row_block, lag_own, preferred_element_type=jnp....  207 us
    dot_general x1, matrix products, shards(): jnp.dot(row_block, lag_own, preferred_element_type=jnp.float32) * inv_root  25.1 us
    dot_general x1, matrix products, shards(): lax.dot_general(row_block, lax.all_gather(signal, 'fsdp', axis=0, tiled=T...  24.6 us
    ppermute x2, starting transfers between devices, from_partner(): return lax.ppermute(block, axis, route)  15.7 us
  transfers between devices with their start and end apart: 5, of which 4 were waited for; matrix products, arithmetic and copies ran while one was open for 5% of the time, Pallas kernels for 0%

commit v1 on v0

--- a/solution.py
+++ b/solution.py
@@ -1,18 +1,25 @@
+import functools
 import math
 
 import jax
 import jax.numpy as jnp
 from jax import lax
+from jax.experimental import pallas as pl
+from jax.experimental.pallas import tpu as pltpu
 from jax.sharding import PartitionSpec as P
 
 D = 2304
 FF = 20480
-
 
 kl_coef = 0.5
 clip_level = 0.15
 step_rate = 8.0
 ema_rate = 0.1
+
+MESH = pl.DeviceIdType.MESH
+VMEM_BYTES = 67_000_000
+RING = 4
+BLOCKS = 32
 
 
 def from_partner(block, axis, distance):
@@ -60,38 +67,581 @@
     return jnp.minimum(1.0, clip_level / (jnp.sqrt(grad_sq / (FF * D)) + 1e-06))
 
 
+def position():
+    me = lax.axis_index("fsdp")
+    return lax.div(me, 16), lax.rem(lax.div(me, 4), 4), lax.rem(me, 4)
+
+
+def wrap(value):
+    return lax.rem(value + 2 * RING, RING)
+
+
+def flat(y, z, x):
+    return y * 16 + z * 4 + x
+
+
+def far_first(index):
+    return jnp.where(index == 0, 2, jnp.where(index == 1, 3, jnp.where(index == 2, 1, 0)))
+
+
+def near_first(index):
+    return jnp.where(index == 2, 3, jnp.where(index == 3, 2, index))
+
+
+def each(count, body):
+    lax.fori_loop(0, count, lambda i, _: (body(i), None)[1], None)
+
+
+def meet_neighbours():
+    y, z, x = position()
+    barrier = pltpu.get_barrier_semaphore()
+    for target in (
+        flat(y, z, wrap(x + 1)),
+        flat(y, z, wrap(x - 1)),
+        flat(y, wrap(z + 1), x),
+        flat(y, wrap(z - 1), x),
+        flat(1 - y, z, x),
+    ):
+        pl.semaphore_signal(
+            barrier,
+            inc=1,
+            device_id=(lax.axis_index("pol"), target),
+            device_id_type=MESH,
+        )
+    pl.semaphore_wait(barrier, 5)
+
+
+def remote(src, dst, send_sem, recv_sem, target):
+    return pltpu.make_async_remote_copy(
+        src_ref=src,
+        dst_ref=dst,
+        send_sem=send_sem,
+        recv_sem=recv_sem,
+        device_id=(lax.axis_index("pol"), target),
+        device_id_type=MESH,
+    )
+
+
+def axes_of(color):
+    _, z, x = position()
+    first = jnp.where(color == 0, x, z)
+    second = jnp.where(color == 0, z, x)
+    return 1 + 3 * color, 4 - 3 * color, first, second
+
+
+def reduce_kernel(
+    gate, up, lag_in, adv, cot,
+    hid_out, wide_out, slim_out,
+    gate_buf, up_buf, lag, hid, wide, slim, wide_in, slim_in,
+    load_sem, lag_sem, out_sem, wide_send, slim_send, wide_recv, slim_recv,
+):
+    y, z, x = position()
+    ff = lag.shape[0]
+    rows = gate_buf.shape[1]
+    half = rows // 2
+    wcols, scols = wide.shape[2], slim.shape[2]
+    inv_root = 1.0 / math.sqrt(FF)
+    lag_copy = pltpu.make_async_copy(lag_in, lag, lag_sem)
+    lag_copy.start()
+
+    def place(j):
+        ey = 1 - lax.rem(j, 2)
+        m = lax.div(j, 2)
+        ez = far_first(lax.div(m, 4))
+        ex = far_first(lax.rem(m, 4))
+        block = flat(lax.rem(y + ey, 2), wrap(z + ez), wrap(x + ex))
+        return ey, ez, ex, block
+
+    def loads(j):
+        slot = lax.rem(j, 2)
+        start = pl.multiple_of(place(j)[3] * rows, rows)
+        return (
+            pltpu.make_async_copy(gate.at[pl.ds(start, rows)], gate_buf.at[slot], load_sem.at[slot, 0]),
+            pltpu.make_async_copy(up.at[pl.ds(start, rows)], up_buf.at[slot], load_sem.at[slot, 1]),
+        )
+
+    for copy in loads(0):
+        copy.start()
+    meet_neighbours()
+
+    def send_wide(cv, block, target, slot):
+        color, part = lax.div(cv, 2), lax.rem(cv, 2)
+        start = pl.multiple_of(block * rows + part * half, half)
+        remote(
+            wide.at[color, pl.ds(start, half)], wide_in.at[cv, slot], wide_send, wide_recv.at[cv, slot], target
+        ).start()
+
+    def send_slim(cv, block, target, slot):
+        color, part = lax.div(cv, 2), lax.rem(cv, 2)
+        start = pl.multiple_of(block * rows + part * half, half)
+        remote(
+            slim.at[color, pl.ds(start, half)], slim_in.at[cv, slot], slim_send, slim_recv.at[cv, slot], target
+        ).start()
+
+    def compute(j):
+        ey, ez, ex, block = place(j)
+        slot = lax.rem(j, 2)
+
+        @pl.when(j + 1 < BLOCKS)
+        def _():
+            for copy in loads(j + 1):
+                copy.start()
+
+        for copy in loads(j):
+            copy.wait()
+        start = pl.multiple_of(block * rows, rows)
+        here = pl.ds(start, rows)
+        hidden = (
+            jax.nn.gelu(gate_buf[slot].astype(jnp.float32), approximate=True)
+            * up_buf[slot].astype(jnp.float32)
+        ).astype(jnp.bfloat16)
+        hid[:, here] = hidden.T
+        pltpu.make_async_copy(hid.at[:, here], hid_out.at[:, here], out_sem).start()
+
+        @pl.when(j == 0)
+        def _():
+            lag_copy.wait()
+
+        for color in range(2):
+            wide[color, here, :] = (
+                jnp.dot(
+                    hidden, lag[:, color * wcols : (color + 1) * wcols], preferred_element_type=jnp.float32
+                )
+                * inv_root
+            ).astype(jnp.bfloat16)
+        for color in range(2):
+            begin = 2 * wcols + color * scols
+            slim[color, here, :] = (
+                jnp.dot(hidden, lag[:, begin : begin + scols], preferred_element_type=jnp.float32) * inv_root
+            ).astype(jnp.bfloat16)
+
+        def leaf_wide(cv):
+            color, s = lax.div(cv, 2), 1 - 2 * lax.rem(cv, 2)
+            sp, sq, p, q = axes_of(color)
+            ep = jnp.where(color == 0, ex, ez)
+            eq = jnp.where(color == 0, ez, ex)
+            u = wrap(s * ep)
+
+            @pl.when(u >= 2)
+            def _():
+                step = jnp.where(u == 2, s, -s)
+                target = y * 16 + wrap(p + step) * sp + q * sq
+                send_wide(cv, block, target, jnp.where(u == 2, 0, 16) + eq * 2 + ey)
+
+        each(4, leaf_wide)
+
+        @pl.when(ey == 1)
+        def _():
+            def leaf_slim(cv):
+                color = lax.div(cv, 2)
+                eq = jnp.where(color == 0, ex, ez)
+                er = jnp.where(color == 0, ez, ex)
+                send_slim(cv, block, flat(1 - y, z, x), eq * 4 + er)
+
+            each(4, leaf_slim)
+
+    each(BLOCKS, compute)
+
+    def gather(total, parts):
+        def tile(i):
+            at = pl.ds(pl.multiple_of(i * 16, 16), 16)
+            value = total[at, :].astype(jnp.float32)
+            for part in parts:
+                value = value + part[at, :].astype(jnp.float32)
+            total[at, :] = value.astype(jnp.bfloat16)
+
+        each(half // 16, tile)
+
+    def take_wide(cv, block, slots):
+        color, part = lax.div(cv, 2), lax.rem(cv, 2)
+        start = pl.multiple_of(block * rows + part * half, half)
+        for slot in slots:
+            remote(
+                wide_in.at[cv, slot], wide_in.at[cv, slot], wide_send, wide_recv.at[cv, slot], flat(1 - y, z, x)
+            ).wait_recv()
+        gather(wide.at[color, pl.ds(start, half)], [wide_in.at[cv, slot] for slot in slots])
+
+    def take_slim(cv, block, slots):
+        color, part = lax.div(cv, 2), lax.rem(cv, 2)
+        start = pl.multiple_of(block * rows + part * half, half)
+        for slot in slots:
+            remote(
+                slim_in.at[cv, slot], slim_in.at[cv, slot], slim_send, slim_recv.at[cv, slot], flat(1 - y, z, x)
+            ).wait_recv()
+        gather(slim.at[color, pl.ds(start, half)], [slim_in.at[cv, slot] for slot in slots])
+
+    def wide_middle(cv, k):
+        color, s = lax.div(cv, 2), 1 - 2 * lax.rem(cv, 2)
+        sp, sq, p, q = axes_of(color)
+        eq, ey = far_first(lax.div(k, 2)), 1 - lax.rem(k, 2)
+        block = lax.rem(y + ey, 2) * 16 + wrap(p + s) * sp + wrap(q + eq) * sq
+        take_wide(cv, block, (eq * 2 + ey,))
+        send_wide(cv, block, y * 16 + wrap(p + s) * sp + q * sq, 8 + eq * 2 + ey)
+
+    def wide_root(cv, k):
+        color, s = lax.div(cv, 2), 1 - 2 * lax.rem(cv, 2)
+        sp, sq, p, q = axes_of(color)
+        eq, ey = far_first(lax.div(k, 2)), 1 - lax.rem(k, 2)
+        v = wrap(s * eq)
+        block = lax.rem(y + ey, 2) * 16 + p * sp + wrap(q + eq) * sq
+        take_wide(cv, block, (8 + eq * 2 + ey, 16 + eq * 2 + ey))
+
+        @pl.when(v == 1)
+        def _():
+            take_wide(cv, block, (24 + ey,))
+
+        @pl.when(v == 0)
+        def _():
+            take_wide(cv, block, (26 + ey, 28 + ey))
+
+        @pl.when(v != 0)
+        def _():
+            step = jnp.where(v == 3, -s, s)
+            slot = jnp.where(v == 2, 24, jnp.where(v == 3, 28, 26)) + ey
+            send_wide(cv, block, y * 16 + p * sp + wrap(q + step) * sq, slot)
+
+        @pl.when((v == 0) & (ey == 1))
+        def _():
+            send_wide(cv, block, flat(1 - y, z, x), 30)
+
+        @pl.when((v == 0) & (ey == 0))
+        def _():
+            take_wide(cv, block, (30,))
+
+    def slim_step(cv, t):
+        color, s = lax.div(cv, 2), 1 - 2 * lax.rem(cv, 2)
+        sq, sr, q, r = axes_of(color)
+        er, eq = far_first(lax.div(t, 4)), far_first(lax.rem(t, 4))
+        v, w = wrap(s * eq), wrap(s * er)
+        block = y * 16 + wrap(q + eq) * sq + wrap(r + er) * sr
+        take_slim(cv, block, (eq * 4 + er,))
+
+        @pl.when(v == 1)
+        def _():
+            take_slim(cv, block, (16 + er,))
+
+        @pl.when(v == 0)
+        def _():
+            take_slim(cv, block, (20 + er, 24 + er))
+
+        @pl.when((v == 0) & (w == 1))
+        def _():
+            take_slim(cv, block, (28,))
+
+        @pl.when((v == 0) & (w == 0))
+        def _():
+            take_slim(cv, block, (29, 30))
+
+        @pl.when((v != 0) | (w != 0))
+        def _():
+            step_q = jnp.where(v == 0, 0, jnp.where(v == 3, -s, s))
+            step_r = jnp.where(v == 0, jnp.where(w == 3, -s, s), 0)
+            slot_q = jnp.where(v == 2, 16, jnp.where(v == 3, 24, 20)) + er
+            slot_r = jnp.where(w == 2, 28, jnp.where(w == 3, 30, 29))
+            target = y * 16 + wrap(q + step_q) * sq + wrap(r + step_r) * sr
+            send_slim(cv, block, target, jnp.where(v == 0, slot_r, slot_q))
+
+    def wave(k):
+        @pl.when(k < 8)
+        def _():
+            each(4, lambda cv: wide_middle(cv, k))
+
+        @pl.when(k > 0)
+        def _():
+            each(4, lambda cv: slim_step(cv, 2 * k - 1))
+
+        @pl.when(k < 8)
+        def _():
+            each(4, lambda cv: slim_step(cv, 2 * k))
+
+        @pl.when(k > 0)
+        def _():
+            each(4, lambda cv: wide_root(cv, k - 1))
+
+    each(9, wave)
+
+    own = pl.ds(pl.multiple_of(flat(y, z, x) * rows, rows), rows)
+    scale = adv[...]
+
+    def finish(source, out, color, begin, width):
+        for i in range(width // 128):
+            lanes = slice(i * 128, (i + 1) * 128)
+            weighted = scale * cot[:, begin + i * 128 : begin + (i + 1) * 128].astype(jnp.float32)
+            gap = source[color, own, lanes].astype(jnp.float32)
+            out[color, :, lanes] = (weighted + kl_coef * gap).astype(jnp.bfloat16)
+
+    for color in range(2):
+        finish(wide, wide_out, color, color * wcols, wcols)
+        finish(slim, slim_out, color, 2 * wcols + color * scols, scols)
+
+    pltpu.make_async_copy(hid, hid_out, out_sem).wait()
+    remote(wide_in, wide_in, wide_send, wide_recv.at[0, 0], flat(1 - y, z, x)).wait_send()
+    remote(slim_in, slim_in, slim_send, slim_recv.at[0, 0], flat(1 - y, z, x)).wait_send()
+
+
+def spread_kernel(
+    hid_in, wide_own, slim_own,
+    grad,
+    hid, wide, slim, total,
+    hid_sem, own_sem, wide_send, slim_send, wide_recv, slim_recv,
+):
+    y, z, x = position()
+    me = flat(y, z, x)
+    rows = wide_own.shape[1]
+    half = rows // 2
+    wcols, scols = wide.shape[2], slim.shape[2]
+    inv_root = 1.0 / math.sqrt(FF)
+    hid_copy = pltpu.make_async_copy(hid_in, hid, hid_sem)
+    hid_copy.start()
+    own = pl.ds(pl.multiple_of(me * rows, rows), rows)
+    own_copies = []
+    for color in range(2):
+        own_copies.append(pltpu.make_async_copy(wide_own.at[color], wide.at[color, own], own_sem.at[color]))
+        own_copies.append(pltpu.make_async_copy(slim_own.at[color], slim.at[color, own], own_sem.at[2 + color]))
+    for copy in own_copies:
+        copy.start()
+    total[...] = jnp.zeros_like(total)
+    for copy in own_copies:
+        copy.wait()
+    meet_neighbours()
+
+    def piece(ref, cv, block):
+        color, part = lax.div(cv, 2), lax.rem(cv, 2)
+        start = pl.multiple_of(block * rows + part * half, half)
+        return ref.at[color, pl.ds(start, half)]
+
+    def send_wide(cv, block, target, slot):
+        here = piece(wide, cv, block)
+        remote(here, here, wide_send, wide_recv.at[cv, slot], target).start()
+
+    def send_slim(cv, block, target, slot):
+        here = piece(slim, cv, block)
+        remote(here, here, slim_send, slim_recv.at[cv, slot], target).start()
+
+    def wait_wide(cv, block, slot):
+        here = piece(wide, cv, block)
+        remote(here, here, wide_send, wide_recv.at[cv, slot], flat(1 - y, z, x)).wait_recv()
+
+    def wait_slim(cv, block, slot):
+        here = piece(slim, cv, block)
+        remote(here, here, slim_send, slim_recv.at[cv, slot], flat(1 - y, z, x)).wait_recv()
+
+    def wide_root(cv, n):
+        color, s = lax.div(cv, 2), 1 - 2 * lax.rem(cv, 2)
+        sp, sq, p, q = axes_of(color)
+        oq, oy = near_first(lax.div(n, 2)), lax.rem(n, 2)
+        b = wrap(s * oq)
+        block = lax.rem(y + oy, 2) * 16 + p * sp + wrap(q - oq) * sq
+        slot = oy * 16 + oq * 4
+
+        @pl.when(n > 0)
+        def _():
+            wait_wide(cv, block, slot)
+
+        @pl.when(n == 0)
+        def _():
+            send_wide(cv, block, flat(1 - y, z, x), 16)
+
+        @pl.when(b <= 1)
+        def _():
+            send_wide(cv, block, y * 16 + p * sp + wrap(q + s) * sq, oy * 16 + wrap(oq + s) * 4)
+
+        @pl.when(b == 0)
+        def _():
+            send_wide(cv, block, y * 16 + p * sp + wrap(q - s) * sq, oy * 16 + wrap(oq - s) * 4)
+
+        send_wide(cv, block, y * 16 + wrap(p + s) * sp + q * sq, slot + wrap(s))
+        send_wide(cv, block, y * 16 + wrap(p - s) * sp + q * sq, slot + wrap(-s))
+
+    def wide_middle(cv, n):
+        color, s = lax.div(cv, 2), 1 - 2 * lax.rem(cv, 2)
+        sp, sq, p, q = axes_of(color)
+        oq, oy = near_first(lax.div(n, 2)), lax.rem(n, 2)
+        block = lax.rem(y + oy, 2) * 16 + wrap(p - s) * sp + wrap(q - oq) * sq
+        slot = oy * 16 + oq * 4
+        wait_wide(cv, block, slot + wrap(s))
+        send_wide(cv, block, y * 16 + wrap(p + s) * sp + q * sq, slot + 2)
+
+    def wide_leaf(cv, n):
+        color, s = lax.div(cv, 2), 1 - 2 * lax.rem(cv, 2)
+        sp, sq, p, q = axes_of(color)
+        oq, oy = near_first(lax.div(n, 2)), lax.rem(n, 2)
+        slot = oy * 16 + oq * 4
+        base = lax.rem(y + oy, 2) * 16 + wrap(q - oq) * sq
+        wait_wide(cv, base + wrap(p + s) * sp, slot + wrap(-s))
+        wait_wide(cv, base + wrap(p + 2) * sp, slot + 2)
+
+    def slim_step(cv, t):
+        color, s = lax.div(cv, 2), 1 - 2 * lax.rem(cv, 2)
+        sq, sr, q, r = axes_of(color)
+        orr, oq = near_first(lax.div(t, 4)), near_first(lax.rem(t, 4))
+        b, c = wrap(s * oq), wrap(s * orr)
+        block = y * 16 + wrap(q - oq) * sq + wrap(r - orr) * sr
+        slot = orr * 4 + oq
+
+        @pl.when(t > 0)
+        def _():
+            wait_slim(cv, block, slot)
+
+        send_slim(cv, block, flat(1 - y, z, x), 16 + slot)
+
+        @pl.when((b == 0) & (c <= 1))
+        def _():
+            send_slim(cv, block, y * 16 + q * sq + wrap(r + s) * sr, wrap(orr + s) * 4)
+
+        @pl.when((b == 0) & (c == 0))
+        def _():
+            send_slim(cv, block, y * 16 + q * sq + wrap(r - s) * sr, wrap(orr - s) * 4)
+
+        @pl.when(b <= 1)
+        def _():
+            send_slim(cv, block, y * 16 + wrap(q + s) * sq + r * sr, orr * 4 + wrap(oq + s))
+
+        @pl.when(b == 0)
+        def _():
+            send_slim(cv, block, y * 16 + wrap(q - s) * sq + r * sr, orr * 4 + wrap(oq - s))
+
+    def slim_leaf(cv, n):
+        color = lax.div(cv, 2)
+        sq, sr, q, r = axes_of(color)
+        orr, oy = near_first(lax.div(n, 2)), lax.rem(n, 2)
+
+        @pl.when(oy == 1)
+        def _():
+            def one(oq):
+                block = (1 - y) * 16 + wrap(q - oq) * sq + wrap(r - orr) * sr
+                wait_slim(cv, block, 16 + orr * 4 + oq)
+
+            each(4, one)
+
+    def multiply(n):
+        each(4, lambda cv: wide_leaf(cv, n))
+        each(4, lambda cv: slim_leaf(cv, n))
+        oo, oy = near_first(lax.div(n, 2)), lax.rem(n, 2)
+        yy = lax.rem(y + oy, 2)
+        for color in range(2):
+            wide_at = color * wcols
+            slim_at = 2 * wcols + color * scols
+            if color == 0:
+                start = pl.multiple_of((yy * 4 + wrap(z - oo)) * 4 * rows, 4 * rows)
+                at = [pl.ds(start, 4 * rows)]
+            else:
+                start = yy * 16 + wrap(x - oo)
+                at = [pl.ds(pl.multiple_of((start + 4 * i) * rows, rows), rows) for i in range(4)]
+            left = jnp.concatenate([hid[:, a] for a in at], axis=1)
+            right = jnp.concatenate([wide[color, a, :] for a in at], axis=0)
+            total[:, wide_at : wide_at + wcols] += jnp.dot(left, right, preferred_element_type=jnp.float32)
+            right = jnp.concatenate([slim[color, a, :] for a in at], axis=0)
+            total[:, slim_at : slim_at + scols] += jnp.dot(left, right, preferred_element_type=jnp.float32)
+
+    def wave(n):
+        @pl.when(n < 8)
+        def _():
+            each(4, lambda cv: wide_root(cv, n))
+
+        @pl.when((n > 0) & (n < 9))
+        def _():
+            each(4, lambda cv: slim_step(cv, 2 * n - 1))
+
+        @pl.when(n < 8)
+        def _():
+            each(4, lambda cv: slim_step(cv, 2 * n))
+
+        @pl.when((n > 0) & (n < 9))
+        def _():
+            each(4, lambda cv: wide_middle(cv, n - 1))
+
+        @pl.when(n == 1)
+        def _():
+            hid_copy.wait()
+
+        @pl.when(n > 1)
+        def _():
+            multiply(n - 2)
+
+    each(10, wave)
+    grad[...] = (total[...] * inv_root).astype(jnp.bfloat16)
+    sent = pl.ds(0, (BLOCKS - 1) * rows)
+    remote(wide.at[:, sent], wide.at[:, sent], wide_send, wide_recv.at[0, 0], flat(1 - y, z, x)).wait_send()
+    remote(slim.at[:, sent], slim.at[:, sent], slim_send, slim_recv.at[0, 0], flat(1 - y, z, x)).wait_send()
+
+
 def shards(gate_pre, up_pre, lag, task, cotangent, buckets, advantages):
     task_own = task[0]
     lag_own = lag[0]
     pol_index = lax.axis_index("pol")
     is_first = pol_index % 2 == 0
     partner_task = from_partner(task_own, "pol", 0)
-    inv_root = 1.0 / math.sqrt(FF)
-    hidden = (
-        jax.nn.gelu(gate_pre[0].astype(jnp.float32), approximate=True)
-        * up_pre[0].astype(jnp.float32)
-    ).astype(jnp.bfloat16)
+    tokens, ff = gate_pre.shape[1:]
+    cols = lag.shape[2]
+    rows = tokens // BLOCKS
+    half = rows // 2
+    wcols, scols = cols // 3, cols // 6
     chosen = (buckets[0][:, None] == jnp.arange(advantages.shape[1])[None, :]).astype(jnp.float32)
     adv_tok = jnp.dot(chosen, advantages[0], precision=lax.Precision.HIGHEST)
-    weighted = adv_tok[:, None] * cotangent[0].astype(jnp.float32)
-    row_block = hidden
-    kl_gap = lax.psum_scatter(
-        (jnp.dot(row_block, lag_own, preferred_element_type=jnp.float32) * inv_root).astype(
-            jnp.bfloat16
+    adv_wide = jnp.broadcast_to(adv_tok[:, None], (rows, 128))
+    any_spec = pl.BlockSpec(memory_space=pl.ANY)
+    vmem_spec = pl.BlockSpec(memory_space=pltpu.VMEM)
+    bf16 = jnp.bfloat16
+    per_stream = [
+        pltpu.SemaphoreType.DMA,
+        pltpu.SemaphoreType.DMA,
+        pltpu.SemaphoreType.DMA((4, BLOCKS)),
+        pltpu.SemaphoreType.DMA((4, BLOCKS)),
+    ]
+    hidden, wide_own, slim_own = pl.pallas_call(
+        reduce_kernel,
+        name="gap_reduce",
+        out_shape=(
+            jax.ShapeDtypeStruct((ff, tokens), bf16),
+            jax.ShapeDtypeStruct((2, rows, wcols), bf16),
+            jax.ShapeDtypeStruct((2, rows, scols), bf16),
         ),
-        "fsdp",
-        scatter_dimension=0,
-        tiled=True,
-    ).astype(jnp.float32)
-    signal = (weighted + kl_coef * kl_gap).astype(jnp.bfloat16)
-    row_block = hidden
-    summed = lax.dot_general(
-        row_block,
-        lax.all_gather(signal, "fsdp", axis=0, tiled=True),
-        (((0,), (0,)), ((), ())),
-        preferred_element_type=jnp.float32,
-    )
-    gradient = (summed * inv_root).astype(jnp.bfloat16)
+        in_specs=[any_spec, any_spec, any_spec, vmem_spec, vmem_spec],
+        out_specs=(any_spec, vmem_spec, vmem_spec),
+        scratch_shapes=[
+            pltpu.VMEM((2, rows, ff), bf16),
+            pltpu.VMEM((2, rows, ff), bf16),
+            pltpu.VMEM((ff, cols), bf16),
+            pltpu.VMEM((ff, tokens), bf16),
+            pltpu.VMEM((2, tokens, wcols), bf16),
+            pltpu.VMEM((2, tokens, scols), bf16),
+            pltpu.VMEM((4, BLOCKS - 1, half, wcols), bf16),
+            pltpu.VMEM((4, BLOCKS - 1, half, scols), bf16),
+            pltpu.SemaphoreType.DMA((2, 2)),
+            pltpu.SemaphoreType.DMA,
+            pltpu.SemaphoreType.DMA,
+            *per_stream,
+        ],
+        compiler_params=pltpu.CompilerParams(
+            collective_id=0, has_side_effects=True, vmem_limit_bytes=VMEM_BYTES
+        ),
+        cost_estimate=pl.CostEstimate(
+            flops=2 * tokens * ff * cols, bytes_accessed=6 * tokens * ff, transcendentals=tokens * ff
+        ),
+    )(gate_pre[0], up_pre[0], lag_own, adv_wide, cotangent[0])
+    gradient = pl.pallas_call(
+        spread_kernel,
+        name="signal_spread",
+        out_shape=jax.ShapeDtypeStruct((ff, cols), bf16),
+        in_specs=[any_spec, any_spec, any_spec],
+        out_specs=vmem_spec,
+        scratch_shapes=[
+            pltpu.VMEM((ff, tokens), bf16),
+            pltpu.VMEM((2, tokens, wcols), bf16),
+            pltpu.VMEM((2, tokens, scols), bf16),
+            pltpu.VMEM((ff, cols), jnp.float32),
+            pltpu.SemaphoreType.DMA,
+            pltpu.SemaphoreType.DMA((4,)),
+            *per_stream,
+        ],
+        compiler_params=pltpu.CompilerParams(
+            collective_id=1, has_side_effects=True, vmem_limit_bytes=VMEM_BYTES
+        ),
+        cost_estimate=pl.CostEstimate(
+            flops=2 * tokens * ff * cols, bytes_accessed=2 * tokens * ff, transcendentals=0
+        ),
+    )(hidden, wide_own, slim_own)
     grad_float = gradient.astype(jnp.float32)
     task_float = task_own.astype(jnp.float32)
     partner_grad = from_partner(gradient, "pol", 0)

time: 547 us -> 258 us (0.47)
  waiting for transfers between devices: 428 us -> 12.3 us
  Pallas kernels: 0 us -> 197 us
  matrix products: 49.9 us -> 0.84 us
  between operations: 22.5 us -> 8.79 us
  starting transfers between devices: 20 us -> 13 us
    all_gather x1 -> x0, waiting for transfers between devices: 209 us -> none  [shards(): lax.all_gather(signal, 'fsdp', axis=0, tiled=True)]
    reduce_scatter x1 -> x0, waiting for transfers between devices: 207 us -> none  [shards(): lax.psum_scatter((jnp.dot(row_block, lag_own, preferred_element_type=jnp....]
    pallas_call x0 -> x2, Pallas kernels: none -> 197 us  [the longest x1 108 us: shards(): pl.pallas_call(reduce_kernel, name='gap_reduce', out_shape=(jax.ShapeDtyp...]
    dot_general x2 -> x0, matrix products: 49.7 us -> none  [the longest x1 25.1 us: shards(): jnp.dot(row_block, lag_own, preferred_element_type=jnp.float32) * inv_root]
    ppermute x2, starting transfers between devices: 15.7 us -> 7.35 us  [from_partner(): return lax.ppermute(block, axis, route)]
  transfers between devices with their start and end apart: 5 -> 3, of which waited for: 4 -> 2; matrix products, arithmetic and copies ran while one was open for 5% -> 1% of each run, Pallas kernels for 0% -> 77%
where the time goes in v1:
time: 258 us; the launch traced here: 257 us
  Pallas kernels  197 us (76%)
  other arithmetic  15 us (6%)
  starting transfers between devices  13 us (5%)
  waiting for transfers between devices  12.3 us (5%)
  local copies, waits for them, and re-layouts  9.98 us (4%)
  between operations  8.79 us (3%)
    pallas_call x1, Pallas kernels, shards(): pl.pallas_call(reduce_kernel, name='gap_reduce', out_shape=(jax.ShapeDtyp...  108 us
    pallas_call x1, Pallas kernels, shards(): pl.pallas_call(spread_kernel, name='signal_spread', out_shape=jax.ShapeDt...  89.3 us
    reduce_sum x1, other arithmetic, shards(): jnp.sum(part_task_float * part_grad_float)  7.54 us
    broadcast_in_dim x1, other arithmetic, shards(): return (new_lag[None], merged[None])  7.45 us
    ppermute x2, starting transfers between devices, from_partner(): return lax.ppermute(block, axis, route)  7.35 us
    all_to_all x1, waiting for transfers between devices, copy_for_each(): lax.all_to_all(jnp.broadcast_to(array[None], (length, *array.shape)), axi...  7.06 us
    concatenate x1, local copies, waits for them, and re-layouts, in_one(): total = taken_together(jnp.concatenate([a.ravel() for a in arrays]), axis)  6.27 us
    all_to_all x1, starting transfers between devices, copy_for_each(): lax.all_to_all(jnp.broadcast_to(array[None], (length, *array.shape)), axi...  5.62 us
  transfers between devices with their start and end apart: 3, of which 2 were waited for; matrix products, arithmetic and copies ran while one was open for 1% of the time, Pallas kernels for 77%

profile of v1, /device:TPU:1, one launch (start us, length us, event | category | flops | bytes accessed | tf_op | source)
XLA Modules:
  0.0 256.8 jit_solution(2761140064327612159)
XLA Ops:
  0.6 0.0 copy-start
  0.6 1.5 collective-permute-start.1
  2.1 0.0 copy-done
  2.1 0.8 convolution_bitcast_fusion
  3.0 0.8 broadcast_in_dim.8.adv
  3.7 107.6 %gap_reduce.1 = (bf16[640,4096]{1,0:T(8,128)(2,1)}, bf16[2,128,768]{2,1,0:T(8,128)(2,1)}, bf16[2,128,384]{2,1,0:T(8,128)(2,1)}) custom-call(bf16[4096,640]{1,0:T(8,128)(2,1)} %bitcast.44, bf16[4096,640]{1,0:T(8,128)(2,1)} %bitcast.45, bf16[640,2304]{1,0:T(8,128)(2,1)} %bitcast.43, f32[128,128]{1,0:T(8,128)} %broadcast_in_dim.8.adv, bf16[128,2304]{1,0:T(8,128)(2,1)} %bitcast.46), custom_call_target="tpu_custom_call" | custom-call | flops 12079595520 | bytes 15728640 | tf_op jit(solution)/shard_map/gap_reduce/pallas_call | solution.py:592
  111.3 89.3 %signal_spread.1 = bf16[640,2304]{1,0:T(8,128)(2,1)} custom-call(bf16[640,4096]{1,0:T(8,128)(2,1)} %get-tuple-element.5.hid_in, bf16[2,128,768]{2,1,0:T(8,128)(2,1)} %get-tuple-element.6.wide_own, bf16[2,128,384]{2,1,0:T(8,128)(2,1)} %get-tuple-element.7.slim_own), custom_call_target="tpu_custom_call" | custom-call | flops 12079595520 | bytes 5242880 | tf_op jit(solution)/shard_map/signal_spread/pallas_call | solution.py:623
  200.7 0.0 copy-start.1
  200.7 5.9 %collective-permute-start = (bf16[640,2304]{1,0:T(8,128)(2,1)}, bf16[640,2304]{1,0:T(8,128)(2,1)S(1)}, u32[]{:S(2)}, u32[]{:S(2)}) collective-permute-start(bf16[640,2304]{1,0:T(8,128)(2,1)} %signal_spread.1), channel_id=1, source_target_pairs={{0,32},{32,0},{64,96},{96,64},{1,33},{33,1},{65,97},{97,65},{2,34}... | collective-permute-start | bytes 8847368 | tf_op jit(solution)/shard_map/ppermute | solution.py:32
  206.6 0.0 collective-permute-done.1
  206.6 5.2 %collective-permute-done = bf16[640,2304]{1,0:T(8,128)(2,1)S(1)} collective-permute-done((bf16[640,2304]{1,0:T(8,128)(2,1)}, bf16[640,2304]{1,0:T(8,128)(2,1)S(1)}, u32[]{:S(2)}, u32[]{:S(2)}) %collective-permute-start) | collective-permute-done | bytes 2949152 | tf_op jit(solution)/shard_map/ppermute | solution.py:32
  211.8 0.0 copy-start.2
  211.8 1.6 copy-done.2
  213.4 7.5 %fusion.15 = (f32[]{:T(128)}, f32[]{:T(128)}, f32[]{:T(128)}, f32[]{:T(128)}, f32[]{:T(128)}, /*index=5*/f32[]{:T(128)}, f32[]{:T(128)}, f32[]{:T(128)}, f32[]{:T(128)}, f32[]{:T(128)}) fusion(bf16[640,2304]{1,0:T(8,128)(2,1)S(1)} %collective-permute-done, bf16[640,2304]{1,0:T(8,128)(2,1)} %collective-permute-done.1, bf16[1,640,2304]{2,1,0:T(8,128)(2,1)} %param.10, ...), kind=kLoop, calls=%fused_computation.29 | loop fusion | flops 35389436 | bytes 11796520 | tf_op jit(solution)/shard_map/reduce_sum | solution.py:661
  221.0 6.3 %concatenate.3 = f32[10]{0:T(128)S(1)} concatenate(f32[1]{0:T(128)} %bitcast.8, f32[1]{0:T(128)} %bitcast.9, f32[1]{0:T(128)} %bitcast.10, f32[1]{0:T(128)} %bitcast.12, f32[1]{0:T(128)} %bitcast.13, f32[1]{0:T(128)} %bitcast.14, f32[1]{0:T(128)} %bitcast.15, f32[1]{0:T(128)} %bitcast.16, f32[1]{0:T(128)} %bitcast.17, f32[1]{0:T(128)} %bitcast.18), dimensions={0} | concatenate | bytes 80 | tf_op jit(solution)/shard_map/concatenate | solution.py:50
  227.2 0.6 broadcast_in_dim.9
  227.8 5.6 %all-to-all-start = ((f32[32,1,10]{2,1,0:T(1,128)}), f32[32,1,10]{2,1,0:T(1,128)S(1)}, u32[]{:S(2)}, u32[]{:S(2)}) async-start(f32[32,1,10]{2,1,0:T(1,128)} %broadcast_in_dim.9), calls=%async_computation | async-start | bytes 32768 | tf_op jit(solution)/shard_map/all_to_all | solution.py:37
  233.5 7.1 %all-to-all-done = f32[32,1,10]{2,1,0:T(1,128)S(1)} async-done(((f32[32,1,10]{2,1,0:T(1,128)}), f32[32,1,10]{2,1,0:T(1,128)S(1)}, u32[]{:S(2)}, u32[]{:S(2)}) %all-to-all-start) | async-done | bytes 1312 | tf_op jit(solution)/shard_map/all_to_all | solution.py:37
  240.5 0.1 reduce_sum.109
  240.6 0.7 fusion.21
  249.4 0.0 copy-done.1
  249.4 7.4 %fusion.17 = (bf16[1,640,2304]{2,1,0:T(8,128)(2,1)}, bf16[1,640,2304]{2,1,0:T(8,128)(2,1)}) fusion(bf16[640,2304]{1,0:T(8,128)(2,1)} %copy-done.2, bf16[640,2304]{1,0:T(8,128)(2,1)} %collective-permute-done.1, bf16[640,2304]{1,0:T(8,128)(2,1)} %signal_spread.1, f32[]{:T(128)S(6)} %mul.142, f32[]{:T(128)S(6)} %select_n.24, f32[]{:T(128)S(6)} %select_n.23, ...), kind=kLoop, calls=%fused_computation.31 | loop fusion | flops 23592960 | bytes 20643856 | tf_op jit(solution)/shard_map/broadcast_in_dim | solution.py:687
Async XLA Ops:
  0.6 1.5 copy-start
  0.6 206.0 %collective-permute-start.1 = (bf16[640,2304]{1,0:T(8,128)(2,1)}, bf16[640,2304]{1,0:T(8,128)(2,1)}, u32[]{:S(2)}, u32[]{:S(2)}) collective-permute-start(bf16[640,2304]{1,0:T(8,128)(2,1)} %bitcast.42), channel_id=1, source_target_pairs={{0,32},{32,0},{64,96},{96,64},{1,33},{33,1},{65,97},{97,65},{2,34}... | collective-permute-start | bytes 8847368 | tf_op jit(solution)/shard_map/ppermute | solution.py:32
  200.7 48.7 %copy-start.1 = (bf16[1,640,2304]{2,1,0:T(8,128)(2,1)S(1)}, bf16[1,640,2304]{2,1,0:T(8,128)(2,1)}, u32[]{:S(2)}) copy-start(bf16[1,640,2304]{2,1,0:T(8,128)(2,1)} %param.10) | copy-start | bytes 8847364
  200.7 11.1 %collective-permute-start = (bf16[640,2304]{1,0:T(8,128)(2,1)}, bf16[640,2304]{1,0:T(8,128)(2,1)S(1)}, u32[]{:S(2)}, u32[]{:S(2)}) collective-permute-start(bf16[640,2304]{1,0:T(8,128)(2,1)} %signal_spread.1), channel_id=1, source_target_pairs={{0,32},{32,0},{64,96},{96,64},{1,33},{33,1},{65,97},{97,65},{2,34}... | collective-permute-start | bytes 8847368 | tf_op jit(solution)/shard_map/ppermute | solution.py:32
  211.8 1.6 copy-start.2
  227.8 12.7 %all-to-all-start = ((f32[32,1,10]{2,1,0:T(1,128)}), f32[32,1,10]{2,1,0:T(1,128)S(1)}, u32[]{:S(2)}, u32[]{:S(2)}) async-start(f32[32,1,10]{2,1,0:T(1,128)} %broadcast_in_dim.9), calls=%async_computation | async-start | bytes 32768 | tf_op jit(solution)/shard_map/all_to_all | solution.py:37

commit v2 on v1

--- a/solution.py
+++ b/solution.py
@@ -30,25 +30,6 @@
         if high != low and high < count:
             route += [(low, high), (high, low)]
     return lax.ppermute(block, axis, route)
-
-
-def copy_for_each(array, axis):
-    length = lax.axis_size(axis)
-    return lax.all_to_all(
-        jnp.broadcast_to(array[None], (length, *array.shape)), axis, 0, 0, tiled=True
-    )
-
-
-def taken_together(array, axis):
-    return copy_for_each(array, axis).sum(axis=0)
-
-
-def in_one(arrays, axis):
-    ends = [0]
-    for a in arrays:
-        ends.append(ends[-1] + a.size)
-    total = taken_together(jnp.concatenate([a.ravel() for a in arrays]), axis)
-    return tuple((total[b:e].reshape(a.shape) for a, b, e in zip(arrays, ends, ends[1:])))
 
 
 def slerp_weights(first_sq, second_sq, cross_dot):
@@ -92,32 +73,52 @@
     lax.fori_loop(0, count, lambda i, _: (body(i), None)[1], None)
 
 
-def meet_neighbours():
+def partner():
+    pol = lax.axis_index("pol")
+    return pol + 1 - 2 * lax.rem(pol, 2)
+
+
+def neighbours():
     y, z, x = position()
+    pol = lax.axis_index("pol")
+    return [
+        (pol, flat(y, z, wrap(x + 1))),
+        (pol, flat(y, z, wrap(x - 1))),
+        (pol, flat(y, wrap(z + 1), x)),
+        (pol, flat(y, wrap(z - 1), x)),
+        (pol, flat(1 - y, z, x)),
+    ]
+
+
+def farther():
+    y, z, x = position()
+    pol = lax.axis_index("pol")
+    return [
+        (pol, flat(y, z, wrap(x + 2))),
+        (pol, flat(y, wrap(z + 2), x)),
+        (partner(), flat(y, z, x)),
+        (partner(), flat(1 - y, z, x)),
+    ]
+
+
+def meet(devices):
     barrier = pltpu.get_barrier_semaphore()
-    for target in (
-        flat(y, z, wrap(x + 1)),
-        flat(y, z, wrap(x - 1)),
-        flat(y, wrap(z + 1), x),
-        flat(y, wrap(z - 1), x),
-        flat(1 - y, z, x),
-    ):
-        pl.semaphore_signal(
-            barrier,
-            inc=1,
-            device_id=(lax.axis_index("pol"), target),
-            device_id_type=MESH,
-        )
-    pl.semaphore_wait(barrier, 5)
+    for device in devices:
+        pl.semaphore_signal(barrier, inc=1, device_id=device, device_id_type=MESH)
+    pl.semaphore_wait(barrier, len(devices))
 
 
 def remote(src, dst, send_sem, recv_sem, target):
+    return remote_to(src, dst, send_sem, recv_sem, (lax.axis_index("pol"), target))
+
+
+def remote_to(src, dst, send_sem, recv_sem, device):
     return pltpu.make_async_remote_copy(
         src_ref=src,
         dst_ref=dst,
         send_sem=send_sem,
         recv_sem=recv_sem,
-        device_id=(lax.axis_index("pol"), target),
+        device_id=device,
         device_id_type=MESH,
     )
 
@@ -132,12 +133,12 @@
 def reduce_kernel(
     gate, up, lag_in, adv, cot,
     hid_out, wide_out, slim_out,
-    gate_buf, up_buf, lag, hid, wide, slim, wide_in, slim_in,
+    gate_buf, up_buf, active, lag, hid, wide, slim, wide_in, slim_in,
     load_sem, lag_sem, out_sem, wide_send, slim_send, wide_recv, slim_recv,
 ):
     y, z, x = position()
     ff = lag.shape[0]
-    rows = gate_buf.shape[1]
+    rows = gate_buf.shape[1] // 2
     half = rows // 2
     wcols, scols = wide.shape[2], slim.shape[2]
     inv_root = 1.0 / math.sqrt(FF)
@@ -145,24 +146,37 @@
     lag_copy.start()
 
     def place(j):
-        ey = 1 - lax.rem(j, 2)
-        m = lax.div(j, 2)
-        ez = far_first(lax.div(m, 4))
-        ex = far_first(lax.rem(m, 4))
-        block = flat(lax.rem(y + ey, 2), wrap(z + ez), wrap(x + ex))
-        return ey, ez, ex, block
+        ez, ex = far_first(lax.div(j, 4)), far_first(lax.rem(j, 4))
+        return ez, ex, flat(1 - y, wrap(z + ez), wrap(x + ex)), flat(y, wrap(z + ez), wrap(x + ex))
 
     def loads(j):
         slot = lax.rem(j, 2)
-        start = pl.multiple_of(place(j)[3] * rows, rows)
-        return (
-            pltpu.make_async_copy(gate.at[pl.ds(start, rows)], gate_buf.at[slot], load_sem.at[slot, 0]),
-            pltpu.make_async_copy(up.at[pl.ds(start, rows)], up_buf.at[slot], load_sem.at[slot, 1]),
-        )
-
-    for copy in loads(0):
-        copy.start()
-    meet_neighbours()
+        copies = []
+        for i, block in enumerate(place(j)[2:]):
+            start = pl.multiple_of(block * rows, rows)
+            there = pl.ds(i * rows, rows)
+            copies.append(
+                pltpu.make_async_copy(gate.at[pl.ds(start, rows)], gate_buf.at[slot, there], load_sem.at[slot, i])
+            )
+            copies.append(
+                pltpu.make_async_copy(up.at[pl.ds(start, rows)], up_buf.at[slot, there], load_sem.at[slot, 2 + i])
+            )
+        return copies
+
+    def activate(j):
+        slot = lax.rem(j, 2)
+        for copy in loads(j):
+            copy.wait()
+        active[slot] = (
+            jax.nn.gelu(gate_buf[slot].astype(jnp.float32), approximate=True)
+            * up_buf[slot].astype(jnp.float32)
+        ).astype(jnp.bfloat16)
+
+    for j in range(2):
+        for copy in loads(j):
+            copy.start()
+    activate(0)
+    meet(neighbours())
 
     def send_wide(cv, block, target, slot):
         color, part = lax.div(cv, 2), lax.rem(cv, 2)
@@ -179,68 +193,64 @@
         ).start()
 
     def compute(j):
-        ey, ez, ex, block = place(j)
+        ez, ex, other, mine = place(j)
         slot = lax.rem(j, 2)
 
-        @pl.when(j + 1 < BLOCKS)
+        @pl.when(j + 2 < BLOCKS // 2)
+        def _():
+            for copy in loads(j + 2):
+                copy.start()
+
+        @pl.when(j + 1 < BLOCKS // 2)
         def _():
             for copy in loads(j + 1):
-                copy.start()
-
-        for copy in loads(j):
-            copy.wait()
-        start = pl.multiple_of(block * rows, rows)
-        here = pl.ds(start, rows)
-        hidden = (
-            jax.nn.gelu(gate_buf[slot].astype(jnp.float32), approximate=True)
-            * up_buf[slot].astype(jnp.float32)
+                copy.wait()
+
+        later = 1 - slot
+        active[later] = (
+            jax.nn.gelu(gate_buf[later].astype(jnp.float32), approximate=True)
+            * up_buf[later].astype(jnp.float32)
         ).astype(jnp.bfloat16)
-        hid[:, here] = hidden.T
-        pltpu.make_async_copy(hid.at[:, here], hid_out.at[:, here], out_sem).start()
-
-        @pl.when(j == 0)
-        def _():
-            lag_copy.wait()
+        hidden = active[slot]
+        places = [pl.ds(pl.multiple_of(block * rows, rows), rows) for block in (other, mine)]
+
+        def product(begin, width):
+            return (
+                jnp.dot(hidden, lag[:, begin : begin + width], preferred_element_type=jnp.float32) * inv_root
+            ).astype(jnp.bfloat16)
 
         for color in range(2):
-            wide[color, here, :] = (
-                jnp.dot(
-                    hidden, lag[:, color * wcols : (color + 1) * wcols], preferred_element_type=jnp.float32
-                )
-                * inv_root
-            ).astype(jnp.bfloat16)
+            value = product(color * wcols, wcols)
+            for i, here in enumerate(places):
+                wide[color, here, :] = value[i * rows : (i + 1) * rows]
         for color in range(2):
-            begin = 2 * wcols + color * scols
-            slim[color, here, :] = (
-                jnp.dot(hidden, lag[:, begin : begin + scols], preferred_element_type=jnp.float32) * inv_root
-            ).astype(jnp.bfloat16)
-
-        def leaf_wide(cv):
+            value = product(2 * wcols + color * scols, scols)
+            for i, here in enumerate(places):
+                slim[color, here, :] = value[i * rows : (i + 1) * rows]
+        for i, here in enumerate(places):
+            hid[:, here] = hidden[i * rows : (i + 1) * rows].T
+            pltpu.make_async_copy(hid.at[:, here], hid_out.at[:, here], out_sem).start()
+
+        def leaf(cv):
             color, s = lax.div(cv, 2), 1 - 2 * lax.rem(cv, 2)
             sp, sq, p, q = axes_of(color)
             ep = jnp.where(color == 0, ex, ez)
             eq = jnp.where(color == 0, ez, ex)
             u = wrap(s * ep)
+            send_slim(cv, other, flat(1 - y, z, x), ep * 4 + eq)
 
             @pl.when(u >= 2)
             def _():
                 step = jnp.where(u == 2, s, -s)
                 target = y * 16 + wrap(p + step) * sp + q * sq
-                send_wide(cv, block, target, jnp.where(u == 2, 0, 16) + eq * 2 + ey)
-
-        each(4, leaf_wide)
-
-        @pl.when(ey == 1)
-        def _():
-            def leaf_slim(cv):
-                color = lax.div(cv, 2)
-                eq = jnp.where(color == 0, ex, ez)
-                er = jnp.where(color == 0, ez, ex)
-                send_slim(cv, block, flat(1 - y, z, x), eq * 4 + er)
-
-            each(4, leaf_slim)
-
-    each(BLOCKS, compute)
+                slot_of = jnp.where(u == 2, 0, 16) + eq * 2
+                send_wide(cv, other, target, slot_of + 1)
+                send_wide(cv, mine, target, slot_of)
+
+        each(4, leaf)
+
+    lag_copy.wait()
+    each(BLOCKS // 2, compute)
 
     def gather(total, parts):
         def tile(i):
@@ -380,10 +390,11 @@
 
 
 def spread_kernel(
-    hid_in, wide_own, slim_own,
-    grad,
-    hid, wide, slim, total,
+    hid_in, wide_own, slim_own, task_in, other_task_in,
+    grad_out, other_grad_out, sums_out,
+    hid, wide, slim, total, task, other_task, grad, other_grad, sums, sums_in,
     hid_sem, own_sem, wide_send, slim_send, wide_recv, slim_recv,
+    task_sem, grad_send, grad_recv, out_sem, sums_send, sums_recv,
 ):
     y, z, x = position()
     me = flat(y, z, x)
@@ -393,6 +404,10 @@
     inv_root = 1.0 / math.sqrt(FF)
     hid_copy = pltpu.make_async_copy(hid_in, hid, hid_sem)
     hid_copy.start()
+    task_copies = [
+        pltpu.make_async_copy(task_in, task, task_sem.at[0]),
+        pltpu.make_async_copy(other_task_in, other_task, task_sem.at[1]),
+    ]
     own = pl.ds(pl.multiple_of(me * rows, rows), rows)
     own_copies = []
     for color in range(2):
@@ -400,10 +415,12 @@
         own_copies.append(pltpu.make_async_copy(slim_own.at[color], slim.at[color, own], own_sem.at[2 + color]))
     for copy in own_copies:
         copy.start()
+    for copy in task_copies:
+        copy.start()
     total[...] = jnp.zeros_like(total)
     for copy in own_copies:
         copy.wait()
-    meet_neighbours()
+    meet(neighbours() + farther())
 
     def piece(ref, cv, block):
         color, part = lax.div(cv, 2), lax.rem(cv, 2)
@@ -554,13 +571,95 @@
         @pl.when(n == 1)
         def _():
             hid_copy.wait()
+            for copy in task_copies:
+                copy.wait()
 
         @pl.when(n > 1)
         def _():
             multiply(n - 2)
 
     each(10, wave)
-    grad[...] = (total[...] * inv_root).astype(jnp.bfloat16)
+
+    ff, cols = grad.shape
+    band = 128
+    tile = 16
+    zero = jnp.zeros((tile, 128), jnp.float32)
+
+    def products(pairs, sums_of, at):
+        done = list(sums_of)
+        for i in range(cols // 128):
+            lanes = slice(i * 128, (i + 1) * 128)
+            read = {}
+            for k, (one, two) in enumerate(pairs):
+                for ref in (one, two):
+                    if id(ref) not in read:
+                        read[id(ref)] = ref[at, lanes].astype(jnp.float32)
+                done[k] = done[k] + read[id(one)] * read[id(two)]
+        return tuple(done)
+
+    def tile_at(i):
+        return pl.ds(pl.multiple_of(i * tile, tile), tile)
+
+    def grad_copy(i):
+        at = pl.ds(i * band, band)
+        return remote_to(grad.at[at], other_grad.at[at], grad_send, grad_recv.at[i], (partner(), me))
+
+    kept = (zero, zero, zero)
+    for i in range(ff // band):
+
+        def settle(k, sums_of):
+            at = tile_at(k)
+            grad[at, :] = (total[at, :] * inv_root).astype(jnp.bfloat16)
+            return products(((grad, grad), (task, grad), (other_task, grad)), sums_of, at)
+
+        kept = lax.fori_loop(i * (band // tile), (i + 1) * (band // tile), settle, kept)
+        grad_copy(i).start()
+        at = pl.ds(i * band, band)
+        pltpu.make_async_copy(grad.at[at], grad_out.at[at], out_sem.at[0]).start()
+    tasks = lax.fori_loop(
+        0,
+        ff // tile,
+        lambda k, sums_of: products(((task, task), (task, other_task)), sums_of, tile_at(k)),
+        (zero, zero),
+    )
+    crossed = (zero,)
+    for i in range(ff // band):
+        grad_copy(i).wait_recv()
+        at = pl.ds(i * band, band)
+        pltpu.make_async_copy(other_grad.at[at], other_grad_out.at[at], out_sem.at[1]).start()
+        crossed = lax.fori_loop(
+            i * (band // tile),
+            (i + 1) * (band // tile),
+            lambda k, sums_of: products(((grad, other_grad),), sums_of, tile_at(k)),
+            crossed,
+        )
+    for i, value in enumerate(kept + tasks + crossed):
+        sums[0, i : i + 1, :] = jnp.sum(value, axis=0, keepdims=True)
+    sums[0, 6:8, :] = jnp.zeros((2, 128), jnp.float32)
+
+    def exchange(source, slots, devices):
+        copies = [
+            remote_to(sums.at[source], sums_in.at[slot], sums_send, sums_recv.at[slot], device)
+            for slot, device in zip(slots, devices)
+        ]
+        for copy in copies:
+            copy.start()
+        for copy in copies:
+            copy.wait_recv()
+
+    pol = lax.axis_index("pol")
+    exchange(0, (0, 1, 2), [(pol, flat(y, z, wrap(x + i))) for i in (1, 2, 3)])
+    sums[1] = sums[0] + sums_in[0] + sums_in[1] + sums_in[2]
+    exchange(1, (3, 4, 5), [(pol, flat(y, wrap(z + i), x)) for i in (1, 2, 3)])
+    sums[2] = sums[1] + sums_in[3] + sums_in[4] + sums_in[5]
+    exchange(2, (6, 7, 8), [(pol, flat(1 - y, z, x)), (partner(), me), (partner(), flat(1 - y, z, x))])
+    sums_out[0] = jnp.broadcast_to(jnp.sum(sums[2] + sums_in[6], axis=1, keepdims=True), (8, 128))
+    sums_out[1] = jnp.broadcast_to(jnp.sum(sums_in[7] + sums_in[8], axis=1, keepdims=True), (8, 128))
+
+    pltpu.make_async_copy(grad, grad_out, out_sem.at[0]).wait()
+    pltpu.make_async_copy(other_grad, other_grad_out, out_sem.at[1]).wait()
+    remote_to(grad, other_grad, grad_send, grad_recv.at[0], (partner(), me)).wait_send()
+    remote_to(sums_in, sums_in, sums_send, sums_recv.at[0], (partner(), me)).wait_send()
     sent = pl.ds(0, (BLOCKS - 1) * rows)
     remote(wide.at[:, sent], wide.at[:, sent], wide_send, wide_recv.at[0, 0], flat(1 - y, z, x)).wait_send()
     remote(slim.at[:, sent], slim.at[:, sent], slim_send, slim_recv.at[0, 0], flat(1 - y, z, x)).wait_send()
@@ -600,15 +699,16 @@
         in_specs=[any_spec, any_spec, any_spec, vmem_spec, vmem_spec],
         out_specs=(any_spec, vmem_spec, vmem_spec),
         scratch_shapes=[
-            pltpu.VMEM((2, rows, ff), bf16),
-            pltpu.VMEM((2, rows, ff), bf16),
+            pltpu.VMEM((2, 2 * rows, ff), bf16),
+            pltpu.VMEM((2, 2 * rows, ff), bf16),
+            pltpu.VMEM((2, 2 * rows, ff), bf16),
             pltpu.VMEM((ff, cols), bf16),
             pltpu.VMEM((ff, tokens), bf16),
             pltpu.VMEM((2, tokens, wcols), bf16),
             pltpu.VMEM((2, tokens, scols), bf16),
             pltpu.VMEM((4, BLOCKS - 1, half, wcols), bf16),
             pltpu.VMEM((4, BLOCKS - 1, half, scols), bf16),
-            pltpu.SemaphoreType.DMA((2, 2)),
+            pltpu.SemaphoreType.DMA((2, 4)),
             pltpu.SemaphoreType.DMA,
             pltpu.SemaphoreType.DMA,
             *per_stream,
@@ -620,20 +720,33 @@
             flops=2 * tokens * ff * cols, bytes_accessed=6 * tokens * ff, transcendentals=tokens * ff
         ),
     )(gate_pre[0], up_pre[0], lag_own, adv_wide, cotangent[0])
-    gradient = pl.pallas_call(
+    gradient, partner_grad, sums = pl.pallas_call(
         spread_kernel,
         name="signal_spread",
-        out_shape=jax.ShapeDtypeStruct((ff, cols), bf16),
-        in_specs=[any_spec, any_spec, any_spec],
-        out_specs=vmem_spec,
+        out_shape=(
+            jax.ShapeDtypeStruct((ff, cols), bf16),
+            jax.ShapeDtypeStruct((ff, cols), bf16),
+            jax.ShapeDtypeStruct((2, 8, 128), jnp.float32),
+        ),
+        in_specs=[any_spec] * 5,
+        out_specs=(any_spec, any_spec, vmem_spec),
         scratch_shapes=[
             pltpu.VMEM((ff, tokens), bf16),
             pltpu.VMEM((2, tokens, wcols), bf16),
             pltpu.VMEM((2, tokens, scols), bf16),
             pltpu.VMEM((ff, cols), jnp.float32),
+            *[pltpu.VMEM((ff, cols), bf16)] * 4,
+            pltpu.VMEM((3, 8, 128), jnp.float32),
+            pltpu.VMEM((9, 8, 128), jnp.float32),
             pltpu.SemaphoreType.DMA,
             pltpu.SemaphoreType.DMA((4,)),
             *per_stream,
+            pltpu.SemaphoreType.DMA((2,)),
+            pltpu.SemaphoreType.DMA,
+            pltpu.SemaphoreType.DMA((ff // 128,)),
+            pltpu.SemaphoreType.DMA((2,)),
+            pltpu.SemaphoreType.DMA,
+            pltpu.SemaphoreType.DMA((9,)),
         ],
         compiler_params=pltpu.CompilerParams(
             collective_id=1, has_side_effects=True, vmem_limit_bytes=VMEM_BYTES
@@ -641,37 +754,17 @@
         cost_estimate=pl.CostEstimate(
             flops=2 * tokens * ff * cols, bytes_accessed=2 * tokens * ff, transcendentals=0
         ),
-    )(hidden, wide_own, slim_own)
+    )(hidden, wide_own, slim_own, task_own, partner_task)
     grad_float = gradient.astype(jnp.float32)
     task_float = task_own.astype(jnp.float32)
-    partner_grad = from_partner(gradient, "pol", 0)
     part_grad_float = partner_grad.astype(jnp.float32)
     part_task_float = partner_task.astype(jnp.float32)
-    dot_sums = in_one(
-        (
-            jnp.sum(grad_float * grad_float),
-            jnp.sum(part_grad_float * part_grad_float),
-            jnp.sum(grad_float * part_grad_float),
-            jnp.sum(task_float * task_float),
-            jnp.sum(part_task_float * part_task_float),
-            jnp.sum(task_float * part_task_float),
-            jnp.sum(task_float * grad_float),
-            jnp.sum(task_float * part_grad_float),
-            jnp.sum(part_task_float * grad_float),
-            jnp.sum(part_task_float * part_grad_float),
-        ),
-        "fsdp",
-    )
-    grad_oo, grad_pp, grad_op, task_oo, task_pp, task_op, tgrad_oo, tgrad_op, tgrad_po, tgrad_pp = (
-        dot_sums
-    )
+    grad_oo, tgrad_oo, tgrad_po, task_oo, task_op, grad_op = (sums[0, i] for i in range(6))
+    grad_pp, tgrad_pp, tgrad_op, task_pp = (sums[1, i] for i in range(4))
     factor_own = clip_factor(grad_oo)
     factor_part = clip_factor(grad_pp)
     scale_own = step_rate * factor_own
     scale_part = step_rate * factor_part
-    update_own = scale_own * grad_float
-    delta_own = task_float - update_own
-    delta_part = part_task_float - scale_part * part_grad_float
     own_total = task_oo - 2.0 * scale_own * tgrad_oo + scale_own * scale_own * grad_oo
     part_total = task_pp - 2.0 * scale_part * tgrad_pp + scale_part * scale_part * grad_pp
     cross_dot = (
@@ -682,6 +775,11 @@
     weight_first, weight_second = slerp_weights(first_sq, second_sq, cross_dot)
     weight_own = jnp.where(is_first, weight_first, weight_second)
     weight_part = jnp.where(is_first, weight_second, weight_first)
+    scalars = lax.optimization_barrier(jnp.stack([weight_own, weight_part, scale_own, scale_part]))
+    weight_own, weight_part, scale_own, scale_part = (scalars[i, 0] for i in range(4))
+    update_own = scale_own * grad_float
+    delta_own = task_float - update_own
+    delta_part = part_task_float - scale_part * part_grad_float
     merged = (weight_own * delta_own + weight_part * delta_part).astype(jnp.bfloat16)
     new_lag = ((1.0 - ema_rate) * (lag_own.astype(jnp.float32) - update_own)).astype(jnp.bfloat16)
     return (new_lag[None], merged[None])

time: 258 us -> 239 us (0.926)
  Pallas kernels: 197 us -> 222 us
  waiting for transfers between devices: 12.3 us -> 0.01 us
  starting transfers between devices: 13 us -> 1.46 us
  local copies, waits for them, and re-layouts: 9.98 us -> 1.38 us
  between operations: 8.79 us -> 0.7 us
    pallas_call x1, Pallas kernels: 89.3 us -> 113 us  [shards(): pl.pallas_call(spread_kernel, name='signal_spread', out_shape=(jax.ShapeD...]
    reduce_sum x2 -> x0, other arithmetic: 7.59 us -> none  [the longest x1 7.54 us: shards(): jnp.sum(part_task_float * part_grad_float)]
    all_to_all x1 -> x0, waiting for transfers between devices: 7.06 us -> none  [copy_for_each(): lax.all_to_all(jnp.broadcast_to(array[None], (length, *array.shape)), axi...]
    concatenate x1 -> x0, local copies, waits for them, and re-layouts: 6.27 us -> none  [in_one(): total = taken_together(jnp.concatenate([a.ravel() for a in arrays]), axis)]
    ppermute x2 -> x1, starting transfers between devices: 7.35 us -> 1.46 us  [from_partner(): return lax.ppermute(block, axis, route)]
    all_to_all x1 -> x0, starting transfers between devices: 5.62 us -> none  [copy_for_each(): lax.all_to_all(jnp.broadcast_to(array[None], (length, *array.shape)), axi...]
    ppermute x2 -> x1, waiting for transfers between devices: 5.21 us -> 0.01 us  [from_partner(): return lax.ppermute(block, axis, route)]
    broadcast_in_dim x1, other arithmetic: 7.45 us -> 10.8 us  [shards(): return (new_lag[None], merged[None])]
  transfers between devices with their start and end apart: 3 -> 1, of which waited for: 2 -> 0; matrix products, arithmetic and copies ran while one was open for 1% -> 1% of each run, Pallas kernels for 77% -> 46%
where the time goes in v2:
time: 239 us
  Pallas kernels  222 us (93%)
  other arithmetic  12.6 us (5%)
    pallas_call x1, Pallas kernels, shards(): pl.pallas_call(spread_kernel, name='signal_spread', out_shape=(jax.ShapeD...  113 us
    pallas_call x1, Pallas kernels, shards(): pl.pallas_call(reduce_kernel, name='gap_reduce', out_shape=(jax.ShapeDtyp...  109 us
    broadcast_in_dim x1, other arithmetic, shards(): return (new_lag[None], merged[None])  10.8 us
  transfers between devices with their start and end apart: 1, of which 0 were waited for; matrix products, arithmetic and copies ran while one was open for 1% of the time, Pallas kernels for 46%

profile of v2, /device:TPU:1, one launch (start us, length us, event | category | flops | bytes accessed | tf_op | source)
XLA Modules:
  0.0 238.6 jit_solution(6565540418505272053)
XLA Ops:
  0.6 0.0 copy-start
  0.6 1.5 collective-permute-start
  2.1 0.0 copy-done
  2.1 0.8 convolution_bitcast_fusion
  3.0 0.8 broadcast_in_dim.6.adv
  3.7 108.6 %gap_reduce.1 = (bf16[640,4096]{1,0:T(8,128)(2,1)}, bf16[2,128,768]{2,1,0:T(8,128)(2,1)}, bf16[2,128,384]{2,1,0:T(8,128)(2,1)}) custom-call(bf16[4096,640]{1,0:T(8,128)(2,1)} %bitcast.107, bf16[4096,640]{1,0:T(8,128)(2,1)} %bitcast.108, bf16[640,2304]{1,0:T(8,128)(2,1)} %bitcast.104, f32[128,128]{1,0:T(8,128)} %broadcast_in_dim.6.adv, ...), custom_call_target="tpu_custom_call" | custom-call | flops 12079595520 | bytes 15728640 | tf_op jit(solution)/shard_map/gap_reduce/pallas_call | solution.py:691
  112.3 0.0 collective-permute-done.other_task_in
  112.3 113.1 %signal_spread.1 = (bf16[640,2304]{1,0:T(8,128)(2,1)}, bf16[640,2304]{1,0:T(8,128)(2,1)}, f32[2,8,128]{2,1,0:T(8,128)}) custom-call(bf16[640,4096]{1,0:T(8,128)(2,1)} %get-tuple-element.8.hid_in, bf16[2,128,768]{2,1,0:T(8,128)(2,1)} %get-tuple-element.9.wide_own, bf16[2,128,384]{2,1,0:T(8,128)(2,1)} %get-tuple-element.10.slim_own, ...), custom_call_target="tpu_custom_call" | custom-call | flops 12079595520 | bytes 5242880 | tf_op jit(solution)/shard_map/signal_spread/pallas_call | solution.py:723
  225.4 0.8 add_divide_fusion
  226.2 0.9 fusion.26
  227.1 0.1 broadcast_select_fusion.1
  227.2 0.6 fusion.27
  227.8 10.8 %fusion.1 = (bf16[1,640,2304]{2,1,0:T(8,128)(2,1)}, bf16[1,640,2304]{2,1,0:T(8,128)(2,1)}) fusion(bf16[640,2304]{1,0:T(8,128)(2,1)} %get-tuple-element.13, bf16[640,2304]{1,0:T(8,128)(2,1)} %collective-permute-done.other_task_in, bf16[640,2304]{1,0:T(8,128)(2,1)} %get-tuple-element.12, f32[]{:T(128)} %bitcast.23, f32[]{:T(128)} %bitcast.22, f32[]{:T(128)} %bitcast.21, ...), kind=kLoop, calls=%fused_computation.4 | loop fusion | flops 23592960 | bytes 20643856 | tf_op jit(solution)/shard_map/broadcast_in_dim | solution.py:785
  (2 shorter events, 0.0 us)
Async XLA Ops:
  0.6 1.5 copy-start
  0.6 111.7 %collective-permute-start = (bf16[640,2304]{1,0:T(8,128)(2,1)}, bf16[640,2304]{1,0:T(8,128)(2,1)}, u32[]{:S(2)}, u32[]{:S(2)}) collective-permute-start(bf16[640,2304]{1,0:T(8,128)(2,1)} %bitcast.105), channel_id=1, source_target_pairs={{0,32},{32,0},{64,96},{96,64},{1,33},{33,1},{65,97},{97,65},{2,34}... | collective-permute-start | bytes 8847368 | tf_op jit(solution)/shard_map/ppermute | solution.py:32

commit v3 on v2

--- a/solution.py
+++ b/solution.py
@@ -37,7 +37,7 @@
     norm_second = jnp.sqrt(second_sq)
     blend = norm_second / (norm_first + norm_second)
     cosine = jnp.clip(cross_dot / (norm_first * norm_second), -1.0, 1.0)
-    opening = jnp.arccos(cosine)
+    opening = jnp.arctan2(jnp.sqrt((1.0 - cosine) * (1.0 + cosine)), cosine)
     sine_val = jnp.sin(opening)
     weight_first = jnp.sin((1.0 - blend) * opening) / sine_val
     weight_second = jnp.sin(blend * opening) / sine_val
@@ -61,12 +61,34 @@
     return y * 16 + z * 4 + x
 
 
+FAR = (2, 3, 1, 0)
+NEAR = (0, 1, 3, 2)
+
+REDUCE_ORDER = ("s0 s4 m0 m1", "m2 m3 m4 m5", "m6 m7 s1 s2", "r0 r1 s5 s6", "s8 s12 s3 r2", "r3 r4 r5 s9", "s7 s10 s13 r6", "s14 s11 r7 s15")
+SPREAD_ORDER = (
+    ("s0 r0 s1 s2", "s4 s8 r1 m0", "s3 r2 s6 s5", "r4 s9 s10 s12", "m1 r3"),
+    ("m2 r5 s7 m4", "s11 s14"),
+    ("m3 s13 r6",),
+    ("m5 r7 s15",),
+    ("m6",),
+    (),
+    ("m7",),
+    (),
+)
+
+
 def far_first(index):
     return jnp.where(index == 0, 2, jnp.where(index == 1, 3, jnp.where(index == 2, 1, 0)))
 
 
 def near_first(index):
     return jnp.where(index == 2, 3, jnp.where(index == 3, 2, index))
+
+
+def steps_of(order, bodies):
+    for step in " ".join(order).split():
+        body, index = bodies[step[0]], int(step[1:])
+        each(4, functools.partial(body, index))
 
 
 def each(count, body):
@@ -280,95 +302,68 @@
             ).wait_recv()
         gather(slim.at[color, pl.ds(start, half)], [slim_in.at[cv, slot] for slot in slots])
 
-    def wide_middle(cv, k):
+    def wide_middle(k, cv):
         color, s = lax.div(cv, 2), 1 - 2 * lax.rem(cv, 2)
         sp, sq, p, q = axes_of(color)
-        eq, ey = far_first(lax.div(k, 2)), 1 - lax.rem(k, 2)
+        eq, ey = FAR[k // 2], 1 - k % 2
         block = lax.rem(y + ey, 2) * 16 + wrap(p + s) * sp + wrap(q + eq) * sq
         take_wide(cv, block, (eq * 2 + ey,))
         send_wide(cv, block, y * 16 + wrap(p + s) * sp + q * sq, 8 + eq * 2 + ey)
 
-    def wide_root(cv, k):
+    def wide_root(k, cv):
         color, s = lax.div(cv, 2), 1 - 2 * lax.rem(cv, 2)
         sp, sq, p, q = axes_of(color)
-        eq, ey = far_first(lax.div(k, 2)), 1 - lax.rem(k, 2)
+        eq, ey = FAR[k // 2], 1 - k % 2
         v = wrap(s * eq)
         block = lax.rem(y + ey, 2) * 16 + p * sp + wrap(q + eq) * sq
-        take_wide(cv, block, (8 + eq * 2 + ey, 16 + eq * 2 + ey))
-
-        @pl.when(v == 1)
-        def _():
-            take_wide(cv, block, (24 + ey,))
-
-        @pl.when(v == 0)
-        def _():
-            take_wide(cv, block, (26 + ey, 28 + ey))
-
-        @pl.when(v != 0)
-        def _():
-            step = jnp.where(v == 3, -s, s)
-            slot = jnp.where(v == 2, 24, jnp.where(v == 3, 28, 26)) + ey
-            send_wide(cv, block, y * 16 + p * sp + wrap(q + step) * sq, slot)
-
-        @pl.when((v == 0) & (ey == 1))
-        def _():
-            send_wide(cv, block, flat(1 - y, z, x), 30)
-
-        @pl.when((v == 0) & (ey == 0))
-        def _():
-            take_wide(cv, block, (30,))
-
-    def slim_step(cv, t):
+        arrived = (8 + eq * 2 + ey, 16 + eq * 2 + ey)
+        if eq == 0:
+            take_wide(cv, block, arrived + (26 + ey, 28 + ey) + ((30,) if ey == 0 else ()))
+            if ey == 1:
+                send_wide(cv, block, flat(1 - y, z, x), 30)
+            return
+        take_wide(cv, block, arrived)
+        if eq != 2:
+
+            @pl.when(v == 1)
+            def _():
+                take_wide(cv, block, (24 + ey,))
+
+        step = jnp.where(v == 3, -s, s)
+        slot = jnp.where(v == 2, 24, jnp.where(v == 3, 28, 26)) + ey
+        send_wide(cv, block, y * 16 + p * sp + wrap(q + step) * sq, slot)
+
+    def slim_step(t, cv):
         color, s = lax.div(cv, 2), 1 - 2 * lax.rem(cv, 2)
         sq, sr, q, r = axes_of(color)
-        er, eq = far_first(lax.div(t, 4)), far_first(lax.rem(t, 4))
+        er, eq = FAR[t // 4], FAR[t % 4]
         v, w = wrap(s * eq), wrap(s * er)
         block = y * 16 + wrap(q + eq) * sq + wrap(r + er) * sr
-        take_slim(cv, block, (eq * 4 + er,))
-
-        @pl.when(v == 1)
-        def _():
-            take_slim(cv, block, (16 + er,))
-
-        @pl.when(v == 0)
-        def _():
-            take_slim(cv, block, (20 + er, 24 + er))
-
-        @pl.when((v == 0) & (w == 1))
-        def _():
-            take_slim(cv, block, (28,))
-
-        @pl.when((v == 0) & (w == 0))
-        def _():
-            take_slim(cv, block, (29, 30))
-
-        @pl.when((v != 0) | (w != 0))
-        def _():
-            step_q = jnp.where(v == 0, 0, jnp.where(v == 3, -s, s))
-            step_r = jnp.where(v == 0, jnp.where(w == 3, -s, s), 0)
-            slot_q = jnp.where(v == 2, 16, jnp.where(v == 3, 24, 20)) + er
-            slot_r = jnp.where(w == 2, 28, jnp.where(w == 3, 30, 29))
-            target = y * 16 + wrap(q + step_q) * sq + wrap(r + step_r) * sr
-            send_slim(cv, block, target, jnp.where(v == 0, slot_r, slot_q))
-
-    def wave(k):
-        @pl.when(k < 8)
-        def _():
-            each(4, lambda cv: wide_middle(cv, k))
-
-        @pl.when(k > 0)
-        def _():
-            each(4, lambda cv: slim_step(cv, 2 * k - 1))
-
-        @pl.when(k < 8)
-        def _():
-            each(4, lambda cv: slim_step(cv, 2 * k))
-
-        @pl.when(k > 0)
-        def _():
-            each(4, lambda cv: wide_root(cv, k - 1))
-
-    each(9, wave)
+        if eq != 0:
+            take_slim(cv, block, (eq * 4 + er,))
+            if eq != 2:
+
+                @pl.when(v == 1)
+                def _():
+                    take_slim(cv, block, (16 + er,))
+
+            step = jnp.where(v == 3, -s, s)
+            slot = jnp.where(v == 2, 16, jnp.where(v == 3, 24, 20)) + er
+            send_slim(cv, block, y * 16 + wrap(q + step) * sq + r * sr, slot)
+            return
+        take_slim(cv, block, (er, 20 + er, 24 + er) + ((29, 30) if er == 0 else ()))
+        if er in (1, 3):
+
+            @pl.when(w == 1)
+            def _():
+                take_slim(cv, block, (28,))
+
+        if er != 0:
+            step = jnp.where(w == 3, -s, s)
+            slot = jnp.where(w == 2, 28, jnp.where(w == 3, 30, 29))
+            send_slim(cv, block, y * 16 + q * sq + wrap(r + step) * sr, slot)
+
+    steps_of(REDUCE_ORDER, {"m": wide_middle, "r": wide_root, "s": slim_step})
 
     own = pl.ds(pl.multiple_of(flat(y, z, x) * rows, rows), rows)
     scale = adv[...]
@@ -390,9 +385,9 @@
 
 
 def spread_kernel(
-    hid_in, wide_own, slim_own, task_in, other_task_in,
-    grad_out, other_grad_out, sums_out,
-    hid, wide, slim, total, task, other_task, grad, other_grad, sums, sums_in,
+    hid_in, wide_own, slim_own, task_in, other_task_in, lag_in,
+    lag_out, merged_out,
+    hid, wide, slim, total, task, other_task, lag, grad, other_grad, sums, sums_in,
     hid_sem, own_sem, wide_send, slim_send, wide_recv, slim_recv,
     task_sem, grad_send, grad_recv, out_sem, sums_send, sums_recv,
 ):
@@ -407,6 +402,7 @@
     task_copies = [
         pltpu.make_async_copy(task_in, task, task_sem.at[0]),
         pltpu.make_async_copy(other_task_in, other_task, task_sem.at[1]),
+        pltpu.make_async_copy(lag_in, lag, task_sem.at[2]),
     ]
     own = pl.ds(pl.multiple_of(me * rows, rows), rows)
     own_copies = []
@@ -443,37 +439,33 @@
         here = piece(slim, cv, block)
         remote(here, here, slim_send, slim_recv.at[cv, slot], flat(1 - y, z, x)).wait_recv()
 
-    def wide_root(cv, n):
+    def wide_root(n, cv):
         color, s = lax.div(cv, 2), 1 - 2 * lax.rem(cv, 2)
         sp, sq, p, q = axes_of(color)
-        oq, oy = near_first(lax.div(n, 2)), lax.rem(n, 2)
+        oq, oy = NEAR[n // 2], n % 2
         b = wrap(s * oq)
         block = lax.rem(y + oy, 2) * 16 + p * sp + wrap(q - oq) * sq
         slot = oy * 16 + oq * 4
-
-        @pl.when(n > 0)
-        def _():
+        if n > 0:
             wait_wide(cv, block, slot)
-
-        @pl.when(n == 0)
-        def _():
+        else:
             send_wide(cv, block, flat(1 - y, z, x), 16)
 
-        @pl.when(b <= 1)
-        def _():
+        def forward():
             send_wide(cv, block, y * 16 + p * sp + wrap(q + s) * sq, oy * 16 + wrap(oq + s) * 4)
 
-        @pl.when(b == 0)
-        def _():
+        if oq == 0:
+            forward()
             send_wide(cv, block, y * 16 + p * sp + wrap(q - s) * sq, oy * 16 + wrap(oq - s) * 4)
-
+        elif oq != 2:
+            pl.when(b == 1)(forward)
         send_wide(cv, block, y * 16 + wrap(p + s) * sp + q * sq, slot + wrap(s))
         send_wide(cv, block, y * 16 + wrap(p - s) * sp + q * sq, slot + wrap(-s))
 
-    def wide_middle(cv, n):
+    def wide_middle(n, cv):
         color, s = lax.div(cv, 2), 1 - 2 * lax.rem(cv, 2)
         sp, sq, p, q = axes_of(color)
-        oq, oy = near_first(lax.div(n, 2)), lax.rem(n, 2)
+        oq, oy = NEAR[n // 2], n % 2
         block = lax.rem(y + oy, 2) * 16 + wrap(p - s) * sp + wrap(q - oq) * sq
         slot = oy * 16 + oq * 4
         wait_wide(cv, block, slot + wrap(s))
@@ -488,35 +480,33 @@
         wait_wide(cv, base + wrap(p + s) * sp, slot + wrap(-s))
         wait_wide(cv, base + wrap(p + 2) * sp, slot + 2)
 
-    def slim_step(cv, t):
+    def slim_step(t, cv):
         color, s = lax.div(cv, 2), 1 - 2 * lax.rem(cv, 2)
         sq, sr, q, r = axes_of(color)
-        orr, oq = near_first(lax.div(t, 4)), near_first(lax.rem(t, 4))
+        orr, oq = NEAR[t // 4], NEAR[t % 4]
         b, c = wrap(s * oq), wrap(s * orr)
         block = y * 16 + wrap(q - oq) * sq + wrap(r - orr) * sr
         slot = orr * 4 + oq
-
-        @pl.when(t > 0)
-        def _():
+        if t > 0:
             wait_slim(cv, block, slot)
-
         send_slim(cv, block, flat(1 - y, z, x), 16 + slot)
 
-        @pl.when((b == 0) & (c <= 1))
-        def _():
+        def forward_third():
             send_slim(cv, block, y * 16 + q * sq + wrap(r + s) * sr, wrap(orr + s) * 4)
 
-        @pl.when((b == 0) & (c == 0))
-        def _():
-            send_slim(cv, block, y * 16 + q * sq + wrap(r - s) * sr, wrap(orr - s) * 4)
-
-        @pl.when(b <= 1)
-        def _():
+        def forward_second():
             send_slim(cv, block, y * 16 + wrap(q + s) * sq + r * sr, orr * 4 + wrap(oq + s))
 
-        @pl.when(b == 0)
-        def _():
+        if oq == 0:
+            if orr == 0:
+                forward_third()
+                send_slim(cv, block, y * 16 + q * sq + wrap(r - s) * sr, wrap(orr - s) * 4)
+            elif orr != 2:
+                pl.when(c == 1)(forward_third)
+            forward_second()
             send_slim(cv, block, y * 16 + wrap(q - s) * sq + r * sr, orr * 4 + wrap(oq - s))
+        elif oq != 2:
+            pl.when(b == 1)(forward_second)
 
     def slim_leaf(cv, n):
         color = lax.div(cv, 2)
@@ -551,39 +541,10 @@
             right = jnp.concatenate([slim[color, a, :] for a in at], axis=0)
             total[:, slim_at : slim_at + scols] += jnp.dot(left, right, preferred_element_type=jnp.float32)
 
-    def wave(n):
-        @pl.when(n < 8)
-        def _():
-            each(4, lambda cv: wide_root(cv, n))
-
-        @pl.when((n > 0) & (n < 9))
-        def _():
-            each(4, lambda cv: slim_step(cv, 2 * n - 1))
-
-        @pl.when(n < 8)
-        def _():
-            each(4, lambda cv: slim_step(cv, 2 * n))
-
-        @pl.when((n > 0) & (n < 9))
-        def _():
-            each(4, lambda cv: wide_middle(cv, n - 1))
-
-        @pl.when(n == 1)
-        def _():
-            hid_copy.wait()
-            for copy in task_copies:
-                copy.wait()
-
-        @pl.when(n > 1)
-        def _():
-            multiply(n - 2)
-
-    each(10, wave)
-
-    ff, cols = grad.shape
     band = 128
     tile = 16
     zero = jnp.zeros((tile, 128), jnp.float32)
+    ff, cols = grad.shape
 
     def products(pairs, sums_of, at):
         done = list(sums_of)
@@ -604,29 +565,38 @@
         at = pl.ds(i * band, band)
         return remote_to(grad.at[at], other_grad.at[at], grad_send, grad_recv.at[i], (partner(), me))
 
-    kept = (zero, zero, zero)
-    for i in range(ff // band):
-
-        def settle(k, sums_of):
-            at = tile_at(k)
-            grad[at, :] = (total[at, :] * inv_root).astype(jnp.bfloat16)
-            return products(((grad, grad), (task, grad), (other_task, grad)), sums_of, at)
-
-        kept = lax.fori_loop(i * (band // tile), (i + 1) * (band // tile), settle, kept)
-        grad_copy(i).start()
-        at = pl.ds(i * band, band)
-        pltpu.make_async_copy(grad.at[at], grad_out.at[at], out_sem.at[0]).start()
+    bodies = {"m": wide_middle, "r": wide_root, "s": slim_step}
+    steps_of(SPREAD_ORDER[0], bodies)
+    hid_copy.wait()
+    for copy in task_copies:
+        copy.wait()
     tasks = lax.fori_loop(
         0,
         ff // tile,
         lambda k, sums_of: products(((task, task), (task, other_task)), sums_of, tile_at(k)),
         (zero, zero),
     )
+
+    def group(n):
+        for i in range(1, len(SPREAD_ORDER)):
+            pl.when(n == i)(functools.partial(steps_of, SPREAD_ORDER[i], bodies))
+        multiply(n)
+
+    each(8, group)
+
+    kept = (zero, zero, zero)
+    for i in range(ff // band):
+
+        def settle(k, sums_of):
+            at = tile_at(k)
+            grad[at, :] = (total[at, :] * inv_root).astype(jnp.bfloat16)
+            return products(((grad, grad), (task, grad), (other_task, grad)), sums_of, at)
+
+        kept = lax.fori_loop(i * (band // tile), (i + 1) * (band // tile), settle, kept)
+        grad_copy(i).start()
     crossed = (zero,)
     for i in range(ff // band):
         grad_copy(i).wait_recv()
-        at = pl.ds(i * band, band)
-        pltpu.make_async_copy(other_grad.at[at], other_grad_out.at[at], out_sem.at[1]).start()
         crossed = lax.fori_loop(
             i * (band // tile),
             (i + 1) * (band // tile),
@@ -653,11 +623,51 @@
     exchange(1, (3, 4, 5), [(pol, flat(y, wrap(z + i), x)) for i in (1, 2, 3)])
     sums[2] = sums[1] + sums_in[3] + sums_in[4] + sums_in[5]
     exchange(2, (6, 7, 8), [(pol, flat(1 - y, z, x)), (partner(), me), (partner(), flat(1 - y, z, x))])
-    sums_out[0] = jnp.broadcast_to(jnp.sum(sums[2] + sums_in[6], axis=1, keepdims=True), (8, 128))
-    sums_out[1] = jnp.broadcast_to(jnp.sum(sums_in[7] + sums_in[8], axis=1, keepdims=True), (8, 128))
-
-    pltpu.make_async_copy(grad, grad_out, out_sem.at[0]).wait()
-    pltpu.make_async_copy(other_grad, other_grad_out, out_sem.at[1]).wait()
+    own_sums = jnp.sum(sums[2] + sums_in[6], axis=1, keepdims=True)
+    part_sums = jnp.sum(sums_in[7] + sums_in[8], axis=1, keepdims=True)
+
+    def spread_row(column, i):
+        return jnp.broadcast_to(column[i : i + 1], (1, 128))
+
+    grad_oo, tgrad_oo, tgrad_po, task_oo, task_op, grad_op = (spread_row(own_sums, i) for i in range(6))
+    grad_pp, tgrad_pp, tgrad_op, task_pp = (spread_row(part_sums, i) for i in range(4))
+    is_first = lax.rem(pol, 2) == 0
+    scale_own = step_rate * clip_factor(grad_oo)
+    scale_part = step_rate * clip_factor(grad_pp)
+    own_total = task_oo - 2.0 * scale_own * tgrad_oo + scale_own * scale_own * grad_oo
+    part_total = task_pp - 2.0 * scale_part * tgrad_pp + scale_part * scale_part * grad_pp
+    cross_dot = (
+        task_op - scale_part * tgrad_op - scale_own * tgrad_po + scale_own * scale_part * grad_op
+    )
+    first_sq = jnp.where(is_first, own_total, part_total)
+    second_sq = jnp.where(is_first, part_total, own_total)
+    weight_first, weight_second = slerp_weights(first_sq, second_sq, cross_dot)
+    weight_own = jnp.where(is_first, weight_first, weight_second)
+    weight_part = jnp.where(is_first, weight_second, weight_first)
+
+    for i in range(ff // band):
+
+        def settle_outputs(k):
+            at = tile_at(k)
+            for i in range(cols // 128):
+                lanes = slice(i * 128, (i + 1) * 128)
+                update = scale_own * grad[at, lanes].astype(jnp.float32)
+                delta_own = task[at, lanes].astype(jnp.float32) - update
+                delta_part = other_task[at, lanes].astype(jnp.float32) - scale_part * other_grad[
+                    at, lanes
+                ].astype(jnp.float32)
+                lag[at, lanes] = ((1.0 - ema_rate) * (lag[at, lanes].astype(jnp.float32) - update)).astype(
+                    jnp.bfloat16
+                )
+                other_grad[at, lanes] = (weight_own * delta_own + weight_part * delta_part).astype(jnp.bfloat16)
+
+        each(band // tile, lambda k: settle_outputs(i * (band // tile) + k))
+        at = pl.ds(i * band, band)
+        pltpu.make_async_copy(lag.at[at], lag_out.at[at], out_sem.at[0]).start()
+        pltpu.make_async_copy(other_grad.at[at], merged_out.at[at], out_sem.at[1]).start()
+
+    pltpu.make_async_copy(lag, lag_out, out_sem.at[0]).wait()
+    pltpu.make_async_copy(other_grad, merged_out, out_sem.at[1]).wait()
     remote_to(grad, other_grad, grad_send, grad_recv.at[0], (partner(), me)).wait_send()
     remote_to(sums_in, sums_in, sums_send, sums_recv.at[0], (partner(), me)).wait_send()
     sent = pl.ds(0, (BLOCKS - 1) * rows)
@@ -668,8 +678,6 @@
 def shards(gate_pre, up_pre, lag, task, cotangent, buckets, advantages):
     task_own = task[0]
     lag_own = lag[0]
-    pol_index = lax.axis_index("pol")
-    is_first = pol_index % 2 == 0
     partner_task = from_partner(task_own, "pol", 0)
     tokens, ff = gate_pre.shape[1:]
     cols = lag.shape[2]
@@ -720,28 +728,27 @@
             flops=2 * tokens * ff * cols, bytes_accessed=6 * tokens * ff, transcendentals=tokens * ff
         ),
     )(gate_pre[0], up_pre[0], lag_own, adv_wide, cotangent[0])
-    gradient, partner_grad, sums = pl.pallas_call(
+    new_lag, merged = pl.pallas_call(
         spread_kernel,
         name="signal_spread",
         out_shape=(
             jax.ShapeDtypeStruct((ff, cols), bf16),
             jax.ShapeDtypeStruct((ff, cols), bf16),
-            jax.ShapeDtypeStruct((2, 8, 128), jnp.float32),
         ),
-        in_specs=[any_spec] * 5,
-        out_specs=(any_spec, any_spec, vmem_spec),
+        in_specs=[any_spec] * 6,
+        out_specs=(any_spec, any_spec),
         scratch_shapes=[
             pltpu.VMEM((ff, tokens), bf16),
             pltpu.VMEM((2, tokens, wcols), bf16),
             pltpu.VMEM((2, tokens, scols), bf16),
             pltpu.VMEM((ff, cols), jnp.float32),
-            *[pltpu.VMEM((ff, cols), bf16)] * 4,
+            *[pltpu.VMEM((ff, cols), bf16)] * 5,
             pltpu.VMEM((3, 8, 128), jnp.float32),
             pltpu.VMEM((9, 8, 128), jnp.float32),
             pltpu.SemaphoreType.DMA,
             pltpu.SemaphoreType.DMA((4,)),
             *per_stream,
-            pltpu.SemaphoreType.DMA((2,)),
+            pltpu.SemaphoreType.DMA((3,)),
             pltpu.SemaphoreType.DMA,
             pltpu.SemaphoreType.DMA((ff // 128,)),
             pltpu.SemaphoreType.DMA((2,)),
@@ -754,34 +761,7 @@
         cost_estimate=pl.CostEstimate(
             flops=2 * tokens * ff * cols, bytes_accessed=2 * tokens * ff, transcendentals=0
         ),
-    )(hidden, wide_own, slim_own, task_own, partner_task)
-    grad_float = gradient.astype(jnp.float32)
-    task_float = task_own.astype(jnp.float32)
-    part_grad_float = partner_grad.astype(jnp.float32)
-    part_task_float = partner_task.astype(jnp.float32)
-    grad_oo, tgrad_oo, tgrad_po, task_oo, task_op, grad_op = (sums[0, i] for i in range(6))
-    grad_pp, tgrad_pp, tgrad_op, task_pp = (sums[1, i] for i in range(4))
-    factor_own = clip_factor(grad_oo)
-    factor_part = clip_factor(grad_pp)
-    scale_own = step_rate * factor_own
-    scale_part = step_rate * factor_part
-    own_total = task_oo - 2.0 * scale_own * tgrad_oo + scale_own * scale_own * grad_oo
-    part_total = task_pp - 2.0 * scale_part * tgrad_pp + scale_part * scale_part * grad_pp
-    cross_dot = (
-        task_op - scale_part * tgrad_op - scale_own * tgrad_po + scale_own * scale_part * grad_op
-    )
-    first_sq = jnp.where(is_first, own_total, part_total)
-    second_sq = jnp.where(is_first, part_total, own_total)
-    weight_first, weight_second = slerp_weights(first_sq, second_sq, cross_dot)
-    weight_own = jnp.where(is_first, weight_first, weight_second)
-    weight_part = jnp.where(is_first, weight_second, weight_first)
-    scalars = lax.optimization_barrier(jnp.stack([weight_own, weight_part, scale_own, scale_part]))
-    weight_own, weight_part, scale_own, scale_part = (scalars[i, 0] for i in range(4))
-    update_own = scale_own * grad_float
-    delta_own = task_float - update_own
-    delta_part = part_task_float - scale_part * part_grad_float
-    merged = (weight_own * delta_own + weight_part * delta_part).astype(jnp.bfloat16)
-    new_lag = ((1.0 - ema_rate) * (lag_own.astype(jnp.float32) - update_own)).astype(jnp.bfloat16)
+    )(hidden, wide_own, slim_own, task_own, partner_task, lag_own)
     return (new_lag[None], merged[None])
 
 

time: 239 us -> 214 us (0.90)
  Pallas kernels: 222 us -> 205 us
  other arithmetic: 12.6 us -> 0 us
  local copies, waits for them, and re-layouts: 1.38 us -> 6.17 us
    pallas_call x1, Pallas kernels: 109 us -> 93.2 us  [shards(): pl.pallas_call(reduce_kernel, name='gap_reduce', out_shape=(jax.ShapeDtyp...]
    broadcast_in_dim x1 -> x0, other arithmetic: 10.8 us -> none  [shards(): return (new_lag[None], merged[None])]
    unnamed x2 -> x6, local copies, waits for them, and re-layouts: 0.01 us -> 5.39 us
  transfers between devices with their start and end apart: 1 -> 1, of which waited for: 0 -> 0; matrix products, arithmetic and copies ran while one was open for 1% -> 1% of each run, Pallas kernels for 46% -> 43%
where the time goes in v3:
time: 214 us
  Pallas kernels  205 us (96%)
  local copies, waits for them, and re-layouts  6.17 us (3%)
    pallas_call x1, Pallas kernels, shards(): pl.pallas_call(spread_kernel, name='signal_spread', out_shape=(jax.ShapeD...  112 us
    pallas_call x1, Pallas kernels, shards(): pl.pallas_call(reduce_kernel, name='gap_reduce', out_shape=(jax.ShapeDtyp...  93.2 us
    unnamed x6, local copies, waits for them, and re-layouts  5.39 us
  transfers between devices with their start and end apart: 1, of which 0 were waited for; matrix products, arithmetic and copies ran while one was open for 1% of the time, Pallas kernels for 43%

profile of v3, /device:TPU:1, one launch (start us, length us, event | category | flops | bytes accessed | tf_op | source)
XLA Modules:
  0.0 214.3 jit_solution(459873094119582091)
XLA Ops:
  0.6 0.0 copy-start
  0.6 1.5 collective-permute-start
  2.1 0.0 copy-done
  2.1 0.8 convolution_bitcast_fusion
  3.0 0.8 broadcast_in_dim.6.adv
  3.7 93.2 %gap_reduce.1 = (bf16[640,4096]{1,0:T(8,128)(2,1)}, bf16[2,128,768]{2,1,0:T(8,128)(2,1)}, bf16[2,128,384]{2,1,0:T(8,128)(2,1)}) custom-call(bf16[4096,640]{1,0:T(8,128)(2,1)} %bitcast.16, bf16[4096,640]{1,0:T(8,128)(2,1)} %bitcast.17, bf16[640,2304]{1,0:T(8,128)(2,1)} %bitcast.18, f32[128,128]{1,0:T(8,128)} %broadcast_in_dim.6.adv, bf16[128,2304]{1,0:T(8,128)(2,1)} %bitcast.22), custom_call_target="tpu_custom_call" | custom-call | flops 12079595520 | bytes 15728640 | tf_op jit(solution)/shard_map/gap_reduce/pallas_call | solution.py:699
  97.0 0.0 collective-permute-done.other_task_in
  97.0 112.0 %signal_spread.1 = (bf16[640,2304]{1,0:T(8,128)(2,1)}, bf16[640,2304]{1,0:T(8,128)(2,1)}) custom-call(bf16[640,4096]{1,0:T(8,128)(2,1)} %get-tuple-element.7.hid_in, bf16[2,128,768]{2,1,0:T(8,128)(2,1)} %get-tuple-element.8.wide_own, bf16[2,128,384]{2,1,0:T(8,128)(2,1)} %get-tuple-element.9.slim_own, bf16[640,2304]{1,0:T(8,128)(2,1)} %bitcast.21, ...), custom_call_target="tpu_custom_call" | custom-call | flops 12079595520 | bytes 5242880 | tf_op jit(solution)/shard_map/signal_spread/pallas_call | solution.py:731
  209.0 0.0 copy-start.1
  209.0 3.8 %copy.11 = bf16[1,640,2304]{2,1,0:T(8,128)(2,1)} copy(bf16[1,640,2304]{2,1,0:T(8,128)(2,1)} %bitcast.15) | data formatting | bytes 5898240
  212.7 0.0 copy-done.1
  212.7 1.6 copy.12
Async XLA Ops:
  0.6 1.5 copy-start
  0.6 96.3 %collective-permute-start = (bf16[640,2304]{1,0:T(8,128)(2,1)}, bf16[640,2304]{1,0:T(8,128)(2,1)}, u32[]{:S(2)}, u32[]{:S(2)}) collective-permute-start(bf16[640,2304]{1,0:T(8,128)(2,1)} %bitcast.20), channel_id=1, source_target_pairs={{0,32},{32,0},{64,96},{96,64},{1,33},{33,1},{65,97},{97,65},{2,34}... | collective-permute-start | bytes 8847368 | tf_op jit(solution)/shard_map/ppermute | solution.py:32
  209.0 3.8 %copy-start.1 = (bf16[640,2304]{1,0:T(8,128)(2,1)S(1)}, bf16[640,2304]{1,0:T(8,128)(2,1)}, u32[]{:S(2)}) copy-start(bf16[640,2304]{1,0:T(8,128)(2,1)} %get-tuple-element.11) | copy-start | bytes 8847364

commit v4 on v3

--- a/solution.py
+++ b/solution.py
@@ -20,16 +20,6 @@
 VMEM_BYTES = 67_000_000
 RING = 4
 BLOCKS = 32
-
-
-def from_partner(block, axis, distance):
-    count = lax.axis_size(axis)
-    route = []
-    for low in range(count):
-        high = low | 1 << distance
-        if high != low and high < count:
-            route += [(low, high), (high, low)]
-    return lax.ppermute(block, axis, route)
 
 
 def slerp_weights(first_sq, second_sq, cross_dot):
@@ -64,15 +54,14 @@
 FAR = (2, 3, 1, 0)
 NEAR = (0, 1, 3, 2)
 
-REDUCE_ORDER = ("s0 s4 m0 m1", "m2 m3 m4 m5", "m6 m7 s1 s2", "r0 r1 s5 s6", "s8 s12 s3 r2", "r3 r4 r5 s9", "s7 s10 s13 r6", "s14 s11 r7 s15")
-SPREAD_ORDER = (
-    ("s0 r0 s1 s2", "s4 s8 r1 m0", "s3 r2 s6 s5", "r4 s9 s10 s12", "m1 r3"),
-    ("m2 r5 s7 m4", "s11 s14"),
-    ("m3 s13 r6",),
-    ("m5 r7 s15",),
-    ("m6",),
+ORDER = (
+    ("s0 m2 s4 m0", "m3 m1 m5 m4", "m6 m7 s1 s2", "s8 s5 r0 s6", "r1 s12 s3 s9", "s10 r4 r2 s13", "s7 s11 s14 r3", "r5 r6 s15 S0", "r7 R0 S1 S2", "S4 S8 R2 M0", "R1 S3 S6 S5", "R4 S9 S10 S12", "M2"),
+    ("R5 M1 R3 S7", "R6 M4 S11 S13", "S14 M5"),
+    ("M3",),
+    ("M6 R7 S15",),
     (),
-    ("m7",),
+    ("M7",),
+    (),
     (),
 )
 
@@ -123,11 +112,13 @@
     ]
 
 
+def greet(devices):
+    for device in devices:
+        pl.semaphore_signal(pltpu.get_barrier_semaphore(), inc=1, device_id=device, device_id_type=MESH)
+
+
 def meet(devices):
-    barrier = pltpu.get_barrier_semaphore()
-    for device in devices:
-        pl.semaphore_signal(barrier, inc=1, device_id=device, device_id_type=MESH)
-    pl.semaphore_wait(barrier, len(devices))
+    pl.semaphore_wait(pltpu.get_barrier_semaphore(), len(devices))
 
 
 def remote(src, dst, send_sem, recv_sem, target):
@@ -152,20 +143,24 @@
     return 1 + 3 * color, 4 - 3 * color, first, second
 
 
-def reduce_kernel(
-    gate, up, lag_in, adv, cot,
-    hid_out, wide_out, slim_out,
+def step_kernel(
+    gate, up, lag_in, task_in, cot, buckets, adv,
+    lag_out, merged_out,
     gate_buf, up_buf, active, lag, hid, wide, slim, wide_in, slim_in,
-    load_sem, lag_sem, out_sem, wide_send, slim_send, wide_recv, slim_recv,
+    total, other_task, grad, other_grad, scale, sums, sums_in,
+    load_sem, task_sem, task_send, task_recv, grad_send, grad_recv, out_sem, sums_send, sums_recv,
+    fold_wide_send, fold_slim_send, fold_wide_recv, fold_slim_recv,
+    wide_send, slim_send, wide_recv, slim_recv, clear,
 ):
     y, z, x = position()
     ff = lag.shape[0]
     rows = gate_buf.shape[1] // 2
+    me = flat(y, z, x)
     half = rows // 2
     wcols, scols = wide.shape[2], slim.shape[2]
     inv_root = 1.0 / math.sqrt(FF)
-    lag_copy = pltpu.make_async_copy(lag_in, lag, lag_sem)
-    lag_copy.start()
+    greet(neighbours() + farther())
+    lag_copy = pltpu.make_async_copy(lag_in, lag, task_sem)
 
     def place(j):
         ez, ex = far_first(lax.div(j, 4)), far_first(lax.rem(j, 4))
@@ -194,24 +189,26 @@
             * up_buf[slot].astype(jnp.float32)
         ).astype(jnp.bfloat16)
 
-    for j in range(2):
-        for copy in loads(j):
-            copy.start()
+    for copy in loads(0):
+        copy.start()
+    lag_copy.start()
+    for copy in loads(1):
+        copy.start()
     activate(0)
-    meet(neighbours())
-
-    def send_wide(cv, block, target, slot):
+    meet(neighbours() + farther())
+
+    def push_wide(cv, block, target, slot):
         color, part = lax.div(cv, 2), lax.rem(cv, 2)
         start = pl.multiple_of(block * rows + part * half, half)
         remote(
-            wide.at[color, pl.ds(start, half)], wide_in.at[cv, slot], wide_send, wide_recv.at[cv, slot], target
+            wide.at[color, pl.ds(start, half)], wide_in.at[cv, slot], fold_wide_send, fold_wide_recv.at[cv, slot], target
         ).start()
 
-    def send_slim(cv, block, target, slot):
+    def push_slim(cv, block, target, slot):
         color, part = lax.div(cv, 2), lax.rem(cv, 2)
         start = pl.multiple_of(block * rows + part * half, half)
         remote(
-            slim.at[color, pl.ds(start, half)], slim_in.at[cv, slot], slim_send, slim_recv.at[cv, slot], target
+            slim.at[color, pl.ds(start, half)], slim_in.at[cv, slot], fold_slim_send, fold_slim_recv.at[cv, slot], target
         ).start()
 
     def compute(j):
@@ -251,7 +248,6 @@
                 slim[color, here, :] = value[i * rows : (i + 1) * rows]
         for i, here in enumerate(places):
             hid[:, here] = hidden[i * rows : (i + 1) * rows].T
-            pltpu.make_async_copy(hid.at[:, here], hid_out.at[:, here], out_sem).start()
 
         def leaf(cv):
             color, s = lax.div(cv, 2), 1 - 2 * lax.rem(cv, 2)
@@ -259,15 +255,15 @@
             ep = jnp.where(color == 0, ex, ez)
             eq = jnp.where(color == 0, ez, ex)
             u = wrap(s * ep)
-            send_slim(cv, other, flat(1 - y, z, x), ep * 4 + eq)
+            push_slim(cv, other, flat(1 - y, z, x), ep * 4 + eq)
 
             @pl.when(u >= 2)
             def _():
                 step = jnp.where(u == 2, s, -s)
                 target = y * 16 + wrap(p + step) * sp + q * sq
                 slot_of = jnp.where(u == 2, 0, 16) + eq * 2
-                send_wide(cv, other, target, slot_of + 1)
-                send_wide(cv, mine, target, slot_of)
+                push_wide(cv, other, target, slot_of + 1)
+                push_wide(cv, mine, target, slot_of)
 
         each(4, leaf)
 
@@ -289,7 +285,7 @@
         start = pl.multiple_of(block * rows + part * half, half)
         for slot in slots:
             remote(
-                wide_in.at[cv, slot], wide_in.at[cv, slot], wide_send, wide_recv.at[cv, slot], flat(1 - y, z, x)
+                wide_in.at[cv, slot], wide_in.at[cv, slot], fold_wide_send, fold_wide_recv.at[cv, slot], flat(1 - y, z, x)
             ).wait_recv()
         gather(wide.at[color, pl.ds(start, half)], [wide_in.at[cv, slot] for slot in slots])
 
@@ -298,19 +294,19 @@
         start = pl.multiple_of(block * rows + part * half, half)
         for slot in slots:
             remote(
-                slim_in.at[cv, slot], slim_in.at[cv, slot], slim_send, slim_recv.at[cv, slot], flat(1 - y, z, x)
+                slim_in.at[cv, slot], slim_in.at[cv, slot], fold_slim_send, fold_slim_recv.at[cv, slot], flat(1 - y, z, x)
             ).wait_recv()
         gather(slim.at[color, pl.ds(start, half)], [slim_in.at[cv, slot] for slot in slots])
 
-    def wide_middle(k, cv):
+    def fold_wide_middle(k, cv):
         color, s = lax.div(cv, 2), 1 - 2 * lax.rem(cv, 2)
         sp, sq, p, q = axes_of(color)
         eq, ey = FAR[k // 2], 1 - k % 2
         block = lax.rem(y + ey, 2) * 16 + wrap(p + s) * sp + wrap(q + eq) * sq
         take_wide(cv, block, (eq * 2 + ey,))
-        send_wide(cv, block, y * 16 + wrap(p + s) * sp + q * sq, 8 + eq * 2 + ey)
-
-    def wide_root(k, cv):
+        push_wide(cv, block, y * 16 + wrap(p + s) * sp + q * sq, 8 + eq * 2 + ey)
+
+    def fold_wide_root(k, cv):
         color, s = lax.div(cv, 2), 1 - 2 * lax.rem(cv, 2)
         sp, sq, p, q = axes_of(color)
         eq, ey = FAR[k // 2], 1 - k % 2
@@ -320,7 +316,7 @@
         if eq == 0:
             take_wide(cv, block, arrived + (26 + ey, 28 + ey) + ((30,) if ey == 0 else ()))
             if ey == 1:
-                send_wide(cv, block, flat(1 - y, z, x), 30)
+                push_wide(cv, block, flat(1 - y, z, x), 30)
             return
         take_wide(cv, block, arrived)
         if eq != 2:
@@ -331,9 +327,9 @@
 
         step = jnp.where(v == 3, -s, s)
         slot = jnp.where(v == 2, 24, jnp.where(v == 3, 28, 26)) + ey
-        send_wide(cv, block, y * 16 + p * sp + wrap(q + step) * sq, slot)
-
-    def slim_step(t, cv):
+        push_wide(cv, block, y * 16 + p * sp + wrap(q + step) * sq, slot)
+
+    def fold_slim_step(t, cv):
         color, s = lax.div(cv, 2), 1 - 2 * lax.rem(cv, 2)
         sq, sr, q, r = axes_of(color)
         er, eq = FAR[t // 4], FAR[t % 4]
@@ -349,7 +345,7 @@
 
             step = jnp.where(v == 3, -s, s)
             slot = jnp.where(v == 2, 16, jnp.where(v == 3, 24, 20)) + er
-            send_slim(cv, block, y * 16 + wrap(q + step) * sq + r * sr, slot)
+            push_slim(cv, block, y * 16 + wrap(q + step) * sq + r * sr, slot)
             return
         take_slim(cv, block, (er, 20 + er, 24 + er) + ((29, 30) if er == 0 else ()))
         if er in (1, 3):
@@ -361,62 +357,71 @@
         if er != 0:
             step = jnp.where(w == 3, -s, s)
             slot = jnp.where(w == 2, 28, jnp.where(w == 3, 30, 29))
-            send_slim(cv, block, y * 16 + q * sq + wrap(r + step) * sr, slot)
-
-    steps_of(REDUCE_ORDER, {"m": wide_middle, "r": wide_root, "s": slim_step})
-
-    own = pl.ds(pl.multiple_of(flat(y, z, x) * rows, rows), rows)
-    scale = adv[...]
-
-    def finish(source, out, color, begin, width):
-        for i in range(width // 128):
-            lanes = slice(i * 128, (i + 1) * 128)
-            weighted = scale * cot[:, begin + i * 128 : begin + (i + 1) * 128].astype(jnp.float32)
-            gap = source[color, own, lanes].astype(jnp.float32)
-            out[color, :, lanes] = (weighted + kl_coef * gap).astype(jnp.bfloat16)
-
-    for color in range(2):
-        finish(wide, wide_out, color, color * wcols, wcols)
-        finish(slim, slim_out, color, 2 * wcols + color * scols, scols)
-
-    pltpu.make_async_copy(hid, hid_out, out_sem).wait()
-    remote(wide_in, wide_in, wide_send, wide_recv.at[0, 0], flat(1 - y, z, x)).wait_send()
-    remote(slim_in, slim_in, slim_send, slim_recv.at[0, 0], flat(1 - y, z, x)).wait_send()
-
-
-def spread_kernel(
-    hid_in, wide_own, slim_own, task_in, other_task_in, lag_in,
-    lag_out, merged_out,
-    hid, wide, slim, total, task, other_task, lag, grad, other_grad, sums, sums_in,
-    hid_sem, own_sem, wide_send, slim_send, wide_recv, slim_recv,
-    task_sem, grad_send, grad_recv, out_sem, sums_send, sums_recv,
-):
-    y, z, x = position()
-    me = flat(y, z, x)
-    rows = wide_own.shape[1]
-    half = rows // 2
-    wcols, scols = wide.shape[2], slim.shape[2]
-    inv_root = 1.0 / math.sqrt(FF)
-    hid_copy = pltpu.make_async_copy(hid_in, hid, hid_sem)
-    hid_copy.start()
-    task_copies = [
-        pltpu.make_async_copy(task_in, task, task_sem.at[0]),
-        pltpu.make_async_copy(other_task_in, other_task, task_sem.at[1]),
-        pltpu.make_async_copy(lag_in, lag, task_sem.at[2]),
-    ]
+            push_slim(cv, block, y * 16 + q * sq + wrap(r + step) * sr, slot)
+
+    task_swap = remote_to(task_in, other_task, task_send, task_recv, (partner(), me))
+    task_swap.start()
+    total[...] = jnp.zeros_like(total)
+
+    buckets_of = lax.broadcasted_iota(jnp.int32, (adv.shape[1], rows), 0)
+    chosen = (buckets_of == buckets[...]).astype(jnp.float32)
+    diagonal = (adv.shape[1], adv.shape[1])
+    adv_column = jnp.sum(
+        jnp.where(
+            lax.broadcasted_iota(jnp.int32, diagonal, 0) == lax.broadcasted_iota(jnp.int32, diagonal, 1),
+            jnp.broadcast_to(adv[...], diagonal),
+            0.0,
+        ),
+        axis=1,
+        keepdims=True,
+    )
+    scale[...] = lax.dot_general(
+        chosen,
+        jnp.broadcast_to(adv_column, (adv.shape[1], 128)),
+        (((0,), (0,)), ((), ())),
+        precision=lax.Precision.HIGHEST,
+        preferred_element_type=jnp.float32,
+    )
     own = pl.ds(pl.multiple_of(me * rows, rows), rows)
-    own_copies = []
-    for color in range(2):
-        own_copies.append(pltpu.make_async_copy(wide_own.at[color], wide.at[color, own], own_sem.at[color]))
-        own_copies.append(pltpu.make_async_copy(slim_own.at[color], slim.at[color, own], own_sem.at[2 + color]))
-    for copy in own_copies:
-        copy.start()
-    for copy in task_copies:
-        copy.start()
-    total[...] = jnp.zeros_like(total)
-    for copy in own_copies:
-        copy.wait()
-    meet(neighbours() + farther())
+
+    def release(kind, received, send_sem, recv_sem):
+        remote(received, received, send_sem, recv_sem.at[0, 0], flat(1 - y, z, x)).wait_send()
+        for device in neighbours():
+            pl.semaphore_signal(clear.at[kind], inc=1, device_id=device, device_id_type=MESH)
+
+    def finish(ref, begin):
+        width = ref.shape[2]
+        for color in range(2):
+            for i in range(width // 128):
+                lanes = slice(i * 128, (i + 1) * 128)
+                first = begin + color * width + i * 128
+                weighted = scale[...] * cot[:, first : first + 128].astype(jnp.float32)
+                gap = ref[color, own, lanes].astype(jnp.float32)
+                ref[color, own, lanes] = (weighted + kl_coef * gap).astype(jnp.bfloat16)
+
+    task = "task"
+    task_pieces = task_in.shape[0] // half
+
+    def load_task():
+        def rows_from(j):
+            at = pl.ds(pl.multiple_of(j * half, half), half)
+            for i in range(task_in.shape[1] // wcols):
+                columns = pl.ds(i * wcols, wcols)
+                pltpu.make_async_copy(task_in.at[at, columns], wide_in.at[i, j], task_sem).start()
+
+        each(task_pieces, rows_from)
+
+    def wait_for_task():
+        everything = wide_in.at[pl.ds(0, task_in.shape[1] // wcols), pl.ds(0, task_pieces)]
+        pltpu.make_async_copy(everything, everything, task_sem).wait()
+
+    def read(ref, k, lanes):
+        if ref is not task:
+            return ref[tile_at(k), lanes].astype(jnp.float32)
+        tiles = half // 16
+        at = pl.ds(pl.multiple_of(lax.rem(k, tiles) * 16, 16), 16)
+        start = lanes.start % wcols
+        return wide_in[lanes.start // wcols, lax.div(k, tiles), at, start : start + 128].astype(jnp.float32)
 
     def piece(ref, cv, block):
         color, part = lax.div(cv, 2), lax.rem(cv, 2)
@@ -521,14 +526,12 @@
 
             each(4, one)
 
-    def multiply(n):
+    def parts_of(n):
         each(4, lambda cv: wide_leaf(cv, n))
         each(4, lambda cv: slim_leaf(cv, n))
         oo, oy = near_first(lax.div(n, 2)), lax.rem(n, 2)
         yy = lax.rem(y + oy, 2)
         for color in range(2):
-            wide_at = color * wcols
-            slim_at = 2 * wcols + color * scols
             if color == 0:
                 start = pl.multiple_of((yy * 4 + wrap(z - oo)) * 4 * rows, 4 * rows)
                 at = [pl.ds(start, 4 * rows)]
@@ -536,73 +539,91 @@
                 start = yy * 16 + wrap(x - oo)
                 at = [pl.ds(pl.multiple_of((start + 4 * i) * rows, rows), rows) for i in range(4)]
             left = jnp.concatenate([hid[:, a] for a in at], axis=1)
-            right = jnp.concatenate([wide[color, a, :] for a in at], axis=0)
-            total[:, wide_at : wide_at + wcols] += jnp.dot(left, right, preferred_element_type=jnp.float32)
-            right = jnp.concatenate([slim[color, a, :] for a in at], axis=0)
-            total[:, slim_at : slim_at + scols] += jnp.dot(left, right, preferred_element_type=jnp.float32)
+            for ref, begin in ((wide, color * wcols), (slim, 2 * wcols + color * scols)):
+                right = jnp.concatenate([ref[color, a, :] for a in at], axis=0)
+                yield begin, jnp.dot(left, right, preferred_element_type=jnp.float32)
 
     band = 128
     tile = 16
     zero = jnp.zeros((tile, 128), jnp.float32)
     ff, cols = grad.shape
 
-    def products(pairs, sums_of, at):
+    def products(pairs, sums_of, k, columns):
         done = list(sums_of)
-        for i in range(cols // 128):
+        for i in range(columns.start // 128, columns.stop // 128):
             lanes = slice(i * 128, (i + 1) * 128)
-            read = {}
-            for k, (one, two) in enumerate(pairs):
+            values = {}
+            for pair, (one, two) in enumerate(pairs):
                 for ref in (one, two):
-                    if id(ref) not in read:
-                        read[id(ref)] = ref[at, lanes].astype(jnp.float32)
-                done[k] = done[k] + read[id(one)] * read[id(two)]
+                    if id(ref) not in values:
+                        values[id(ref)] = read(ref, k, lanes)
+                done[pair] = done[pair] + values[id(one)] * values[id(two)]
         return tuple(done)
+
+    def sum_products(pairs, start, columns):
+        return lax.fori_loop(
+            0, ff // tile, lambda k, sums_of: products(pairs, sums_of, k, columns), start
+        )
 
     def tile_at(i):
         return pl.ds(pl.multiple_of(i * tile, tile), tile)
 
-    def grad_copy(i):
-        at = pl.ds(i * band, band)
-        return remote_to(grad.at[at], other_grad.at[at], grad_send, grad_recv.at[i], (partner(), me))
-
-    bodies = {"m": wide_middle, "r": wide_root, "s": slim_step}
-    steps_of(SPREAD_ORDER[0], bodies)
-    hid_copy.wait()
-    for copy in task_copies:
-        copy.wait()
-    tasks = lax.fori_loop(
-        0,
-        ff // tile,
-        lambda k, sums_of: products(((task, task), (task, other_task)), sums_of, tile_at(k)),
-        (zero, zero),
-    )
+    column_parts = [
+        slice(0, wcols),
+        slice(2 * wcols, 2 * wcols + scols),
+        slice(wcols, 2 * wcols),
+        slice(2 * wcols + scols, cols),
+    ]
+
+    def grad_copy(part):
+        columns = pl.ds(column_parts[part].start, column_parts[part].stop - column_parts[part].start)
+        return remote_to(
+            grad.at[:, columns], other_grad.at[:, columns], grad_send, grad_recv.at[part], (partner(), me)
+        )
+
+    bodies = {
+        "m": fold_wide_middle,
+        "r": fold_wide_root,
+        "s": fold_slim_step,
+        "M": wide_middle,
+        "R": wide_root,
+        "S": slim_step,
+    }
+    for step in " ".join(ORDER[0]).split():
+        if step == "R0":
+            pl.semaphore_wait(clear.at[0], 5)
+        if step == "S0":
+            pl.semaphore_wait(clear.at[1], 5)
+        steps_of((step,), bodies)
+        if step == "r7":
+            release(0, wide_in, fold_wide_send, fold_wide_recv)
+            finish(wide, 0)
+            load_task()
+        if step == "s15":
+            release(1, slim_in, fold_slim_send, fold_slim_recv)
+            finish(slim, 2 * wcols)
+    wait_for_task()
+    task_swap.wait_recv()
+    tasks = sum_products(((task, task), (task, other_task)), (zero, zero), slice(0, cols))
 
     def group(n):
-        for i in range(1, len(SPREAD_ORDER)):
-            pl.when(n == i)(functools.partial(steps_of, SPREAD_ORDER[i], bodies))
-        multiply(n)
-
-    each(8, group)
-
+        for i in range(1, len(ORDER) - 1):
+            pl.when(n == i)(functools.partial(steps_of, ORDER[i], bodies))
+        for begin, product in parts_of(n):
+            total[:, begin : begin + product.shape[1]] += product
+
+    each(7, group)
+    steps_of(ORDER[7], bodies)
     kept = (zero, zero, zero)
-    for i in range(ff // band):
-
-        def settle(k, sums_of):
-            at = tile_at(k)
-            grad[at, :] = (total[at, :] * inv_root).astype(jnp.bfloat16)
-            return products(((grad, grad), (task, grad), (other_task, grad)), sums_of, at)
-
-        kept = lax.fori_loop(i * (band // tile), (i + 1) * (band // tile), settle, kept)
-        grad_copy(i).start()
+    for part, (begin, product) in enumerate(parts_of(7)):
+        columns = column_parts[part]
+        grad[:, columns] = ((total[:, columns] + product) * inv_root).astype(jnp.bfloat16)
+        grad_copy(part).start()
+        kept = sum_products(((grad, grad), (task, grad), (other_task, grad)), kept, columns)
     crossed = (zero,)
-    for i in range(ff // band):
-        grad_copy(i).wait_recv()
-        crossed = lax.fori_loop(
-            i * (band // tile),
-            (i + 1) * (band // tile),
-            lambda k, sums_of: products(((grad, other_grad),), sums_of, tile_at(k)),
-            crossed,
-        )
+    for part in range(4):
+        grad_copy(part).wait_recv()
+        crossed = sum_products(((grad, other_grad),), crossed, column_parts[part])
     for i, value in enumerate(kept + tasks + crossed):
         sums[0, i : i + 1, :] = jnp.sum(value, axis=0, keepdims=True)
     sums[0, 6:8, :] = jnp.zeros((2, 128), jnp.float32)
@@ -652,7 +673,7 @@
             for i in range(cols // 128):
                 lanes = slice(i * 128, (i + 1) * 128)
                 update = scale_own * grad[at, lanes].astype(jnp.float32)
-                delta_own = task[at, lanes].astype(jnp.float32) - update
+                delta_own = read(task, k, lanes) - update
                 delta_part = other_task[at, lanes].astype(jnp.float32) - scale_part * other_grad[
                     at, lanes
                 ].astype(jnp.float32)
@@ -668,6 +689,7 @@
 
     pltpu.make_async_copy(lag, lag_out, out_sem.at[0]).wait()
     pltpu.make_async_copy(other_grad, merged_out, out_sem.at[1]).wait()
+    task_swap.wait_send()
     remote_to(grad, other_grad, grad_send, grad_recv.at[0], (partner(), me)).wait_send()
     remote_to(sums_in, sums_in, sums_send, sums_recv.at[0], (partner(), me)).wait_send()
     sent = pl.ds(0, (BLOCKS - 1) * rows)
@@ -676,92 +698,55 @@
 
 
 def shards(gate_pre, up_pre, lag, task, cotangent, buckets, advantages):
-    task_own = task[0]
-    lag_own = lag[0]
-    partner_task = from_partner(task_own, "pol", 0)
     tokens, ff = gate_pre.shape[1:]
     cols = lag.shape[2]
     rows = tokens // BLOCKS
     half = rows // 2
     wcols, scols = cols // 3, cols // 6
-    chosen = (buckets[0][:, None] == jnp.arange(advantages.shape[1])[None, :]).astype(jnp.float32)
-    adv_tok = jnp.dot(chosen, advantages[0], precision=lax.Precision.HIGHEST)
-    adv_wide = jnp.broadcast_to(adv_tok[:, None], (rows, 128))
     any_spec = pl.BlockSpec(memory_space=pl.ANY)
     vmem_spec = pl.BlockSpec(memory_space=pltpu.VMEM)
     bf16 = jnp.bfloat16
-    per_stream = [
-        pltpu.SemaphoreType.DMA,
-        pltpu.SemaphoreType.DMA,
-        pltpu.SemaphoreType.DMA((4, BLOCKS)),
-        pltpu.SemaphoreType.DMA((4, BLOCKS)),
-    ]
-    hidden, wide_own, slim_own = pl.pallas_call(
-        reduce_kernel,
-        name="gap_reduce",
-        out_shape=(
-            jax.ShapeDtypeStruct((ff, tokens), bf16),
-            jax.ShapeDtypeStruct((2, rows, wcols), bf16),
-            jax.ShapeDtypeStruct((2, rows, scols), bf16),
-        ),
-        in_specs=[any_spec, any_spec, any_spec, vmem_spec, vmem_spec],
-        out_specs=(any_spec, vmem_spec, vmem_spec),
+    dma = pltpu.SemaphoreType.DMA
+    per_stream = [dma, dma, dma((4, BLOCKS)), dma((4, BLOCKS))]
+    new_lag, merged = pl.pallas_call(
+        step_kernel,
+        name="policy_step",
+        out_shape=(jax.ShapeDtypeStruct((ff, cols), bf16), jax.ShapeDtypeStruct((ff, cols), bf16)),
+        in_specs=[any_spec] * 4 + [vmem_spec] * 3,
+        out_specs=(any_spec, any_spec),
         scratch_shapes=[
-            pltpu.VMEM((2, 2 * rows, ff), bf16),
-            pltpu.VMEM((2, 2 * rows, ff), bf16),
-            pltpu.VMEM((2, 2 * rows, ff), bf16),
+            *[pltpu.VMEM((2, 2 * rows, ff), bf16)] * 3,
             pltpu.VMEM((ff, cols), bf16),
             pltpu.VMEM((ff, tokens), bf16),
             pltpu.VMEM((2, tokens, wcols), bf16),
             pltpu.VMEM((2, tokens, scols), bf16),
             pltpu.VMEM((4, BLOCKS - 1, half, wcols), bf16),
             pltpu.VMEM((4, BLOCKS - 1, half, scols), bf16),
-            pltpu.SemaphoreType.DMA((2, 4)),
-            pltpu.SemaphoreType.DMA,
-            pltpu.SemaphoreType.DMA,
+            pltpu.VMEM((ff, cols), jnp.float32),
+            *[pltpu.VMEM((ff, cols), bf16)] * 3,
+            pltpu.VMEM((rows, 128), jnp.float32),
+            pltpu.VMEM((3, 8, 128), jnp.float32),
+            pltpu.VMEM((9, 8, 128), jnp.float32),
+            dma((2, 4)),
+            dma,
+            dma,
+            dma,
+            dma,
+            dma((4,)),
+            dma((2,)),
+            dma,
+            dma((9,)),
             *per_stream,
+            *per_stream,
+            pltpu.SemaphoreType.REGULAR((2,)),
         ],
         compiler_params=pltpu.CompilerParams(
             collective_id=0, has_side_effects=True, vmem_limit_bytes=VMEM_BYTES
         ),
         cost_estimate=pl.CostEstimate(
-            flops=2 * tokens * ff * cols, bytes_accessed=6 * tokens * ff, transcendentals=tokens * ff
+            flops=4 * tokens * ff * cols, bytes_accessed=6 * tokens * ff, transcendentals=tokens * ff
         ),
-    )(gate_pre[0], up_pre[0], lag_own, adv_wide, cotangent[0])
-    new_lag, merged = pl.pallas_call(
-        spread_kernel,
-        name="signal_spread",
-        out_shape=(
-            jax.ShapeDtypeStruct((ff, cols), bf16),
-            jax.ShapeDtypeStruct((ff, cols), bf16),
-        ),
-        in_specs=[any_spec] * 6,
-        out_specs=(any_spec, any_spec),
-        scratch_shapes=[
-            pltpu.VMEM((ff, tokens), bf16),
-            pltpu.VMEM((2, tokens, wcols), bf16),
-            pltpu.VMEM((2, tokens, scols), bf16),
-            pltpu.VMEM((ff, cols), jnp.float32),
-            *[pltpu.VMEM((ff, cols), bf16)] * 5,
-            pltpu.VMEM((3, 8, 128), jnp.float32),
-            pltpu.VMEM((9, 8, 128), jnp.float32),
-            pltpu.SemaphoreType.DMA,
-            pltpu.SemaphoreType.DMA((4,)),
-            *per_stream,
-            pltpu.SemaphoreType.DMA((3,)),
-            pltpu.SemaphoreType.DMA,
-            pltpu.SemaphoreType.DMA((ff // 128,)),
-            pltpu.SemaphoreType.DMA((2,)),
-            pltpu.SemaphoreType.DMA,
-            pltpu.SemaphoreType.DMA((9,)),
-        ],
-        compiler_params=pltpu.CompilerParams(
-            collective_id=1, has_side_effects=True, vmem_limit_bytes=VMEM_BYTES
-        ),
-        cost_estimate=pl.CostEstimate(
-            flops=2 * tokens * ff * cols, bytes_accessed=2 * tokens * ff, transcendentals=0
-        ),
-    )(hidden, wide_own, slim_own, task_own, partner_task, lag_own)
+    )(gate_pre[0], up_pre[0], lag[0], task[0], cotangent[0], buckets, advantages)
     return (new_lag[None], merged[None])
 
 

time: 214 us -> 206 us (0.963)
  Pallas kernels: 205 us -> 199 us
    pallas_call x2 -> x1, Pallas kernels: 205 us -> 199 us  [shards(): pl.pallas_call(step_kernel, name='policy_step', out_shape=(jax.ShapeDtype...]
    unnamed x6 -> x4, local copies, waits for them, and re-layouts: 5.39 us -> 5.38 us
  transfers between devices with their start and end apart: 1 -> 0, of which waited for: 0 -> 0; matrix products, arithmetic and copies ran while one was open for 1% -> 0% of each run, Pallas kernels for 43% -> 0%
where the time goes in v4:
time: 206 us; the launch traced here: 205 us
  Pallas kernels  199 us (97%)
  local copies, waits for them, and re-layouts  5.38 us (3%)
    pallas_call x1, Pallas kernels, shards(): pl.pallas_call(step_kernel, name='policy_step', out_shape=(jax.ShapeDtype...  199 us
    unnamed x4, local copies, waits for them, and re-layouts  5.38 us

profile of v4, /device:TPU:1, one launch (start us, length us, event | category | flops | bytes accessed | tf_op | source)
XLA Modules:
  0.0 205.4 jit_solution(11519635245226186474)
XLA Ops:
  0.6 199.4 %policy_step.1 = (bf16[640,2304]{1,0:T(8,128)(2,1)}, bf16[640,2304]{1,0:T(8,128)(2,1)}) custom-call(bf16[4096,640]{1,0:T(8,128)(2,1)} %bitcast.9, bf16[4096,640]{1,0:T(8,128)(2,1)} %bitcast.10, bf16[640,2304]{1,0:T(8,128)(2,1)} %bitcast.11, bf16[640,2304]{1,0:T(8,128)(2,1)} %bitcast.12, bf16[128,2304]{1,0:T(8,128)(2,1)} %bitcast.13, s32[1,128]{1,0:T(1,128)} %buckets.1, ...), custom_call_target="tpu_custom_call" | custom-call | flops 24159191040 | bytes 15728640 | tf_op jit(solution)/shard_map/policy_step/pallas_call | solution.py:711
  200.0 0.0 copy-start
  200.0 3.8 %copy.11 = bf16[1,640,2304]{2,1,0:T(8,128)(2,1)} copy(bf16[1,640,2304]{2,1,0:T(8,128)(2,1)} %bitcast.8) | data formatting | bytes 5898240
  203.8 0.0 copy-done
  203.8 1.6 copy.12
Async XLA Ops:
  200.0 3.8 %copy-start = (bf16[640,2304]{1,0:T(8,128)(2,1)S(1)}, bf16[640,2304]{1,0:T(8,128)(2,1)}, u32[]{:S(2)}) copy-start(bf16[640,2304]{1,0:T(8,128)(2,1)} %get-tuple-element.5) | copy-start | bytes 8847364

commit v5 on v4

--- a/solution.py
+++ b/solution.py
@@ -55,15 +55,16 @@
 NEAR = (0, 1, 3, 2)
 
 ORDER = (
-    ("s0 m2 s4 m0", "m3 m1 m5 m4", "m6 m7 s1 s2", "s8 s5 r0 s6", "r1 s12 s3 s9", "s10 r4 r2 s13", "s7 s11 s14 r3", "r5 r6 s15 S0", "r7 R0 S1 S2", "S4 S8 R2 M0", "R1 S3 S6 S5", "R4 S9 S10 S12", "M2"),
-    ("R5 M1 R3 S7", "R6 M4 S11 S13", "S14 M5"),
-    ("M3",),
-    ("M6 R7 S15",),
+    ("s0 s4 m0 m2", "m5 m3 m1 m4", "m6 m7 s1 s5", "s8 s2 r0 s6", "r1 s12 s10 s3", "s9 r2 r4 s13", "s7 s14 s11 r3", "r5 r6 s15 S0", "r7 R0 S1 S2", "S4 S8 M0 R1", "R4 R2 S3 S6", "S5 S10 S9 S12"),
+    ("M1 R3 R5 M4", "R6 M2 S7 S11", "S13 S14"),
+    ("M3 M5 R7",),
+    ("M6",),
+    ("S15",),
     (),
     ("M7",),
     (),
-    (),
 )
+GROUPS = (0, 1, 4, 2, 3, 5, 6, 7)
 
 
 def far_first(index):
@@ -101,14 +102,19 @@
     ]
 
 
-def farther():
+def plane():
     y, z, x = position()
-    pol = lax.axis_index("pol")
+    offsets = sorted(((i, j) for i in range(4) for j in range(4) if i or j), key=lambda o: o.count(2) * 4 - o.count(0))
+    offsets.reverse()
+    return [(lax.axis_index("pol"), flat(y, wrap(z + i), wrap(x + j))) for i, j in offsets]
+
+
+def across():
+    y, z, x = position()
     return [
-        (pol, flat(y, z, wrap(x + 2))),
-        (pol, flat(y, wrap(z + 2), x)),
+        (partner(), flat(1 - y, z, x)),
+        (lax.axis_index("pol"), flat(1 - y, z, x)),
         (partner(), flat(y, z, x)),
-        (partner(), flat(1 - y, z, x)),
     ]
 
 
@@ -148,19 +154,20 @@
     lag_out, merged_out,
     gate_buf, up_buf, active, lag, hid, wide, slim, wide_in, slim_in,
     total, other_task, grad, other_grad, scale, sums, sums_in,
-    load_sem, task_sem, task_send, task_recv, grad_send, grad_recv, out_sem, sums_send, sums_recv,
+    load_sem, lag_sem, task_sem, task_send, task_recv, grad_send, grad_recv, out_sem, sums_send, sums_recv,
     fold_wide_send, fold_slim_send, fold_wide_recv, fold_slim_recv,
     wide_send, slim_send, wide_recv, slim_recv, clear,
 ):
     y, z, x = position()
-    ff = lag.shape[0]
     rows = gate_buf.shape[1] // 2
     me = flat(y, z, x)
     half = rows // 2
     wcols, scols = wide.shape[2], slim.shape[2]
     inv_root = 1.0 / math.sqrt(FF)
-    greet(neighbours() + farther())
-    lag_copy = pltpu.make_async_copy(lag_in, lag, task_sem)
+    greet(plane() + across())
+    lag_copies = []
+    for i, columns in enumerate((pl.ds(0, wcols), pl.ds(wcols, wcols), pl.ds(2 * wcols, 2 * scols))):
+        lag_copies.append(pltpu.make_async_copy(lag_in.at[:, columns], lag.at[:, columns], lag_sem.at[i]))
 
     def place(j):
         ez, ex = far_first(lax.div(j, 4)), far_first(lax.rem(j, 4))
@@ -189,13 +196,9 @@
             * up_buf[slot].astype(jnp.float32)
         ).astype(jnp.bfloat16)
 
-    for copy in loads(0):
-        copy.start()
-    lag_copy.start()
-    for copy in loads(1):
+    for copy in loads(0) + lag_copies + loads(1):
         copy.start()
     activate(0)
-    meet(neighbours() + farther())
 
     def push_wide(cv, block, target, slot):
         color, part = lax.div(cv, 2), lax.rem(cv, 2)
@@ -211,10 +214,54 @@
             slim.at[color, pl.ds(start, half)], slim_in.at[cv, slot], fold_slim_send, fold_slim_recv.at[cv, slot], target
         ).start()
 
+    def product(hidden, begin, width):
+        return (
+            jnp.dot(hidden, lag[:, begin : begin + width], preferred_element_type=jnp.float32) * inv_root
+        ).astype(jnp.bfloat16)
+
+    def keep_product(j, ref, color, begin):
+        value = product(active[lax.rem(j, 2)], begin, ref.shape[2])
+        for i, block in enumerate(place(j)[2:]):
+            here = pl.ds(pl.multiple_of(block * rows, rows), rows)
+            ref[color, here, :] = value[i * rows : (i + 1) * rows]
+
+    def keep_hidden(j):
+        hidden = active[lax.rem(j, 2)]
+        for i, block in enumerate(place(j)[2:]):
+            here = pl.ds(pl.multiple_of(block * rows, rows), rows)
+            hid[:, here] = hidden[i * rows : (i + 1) * rows].T
+
+    def activate_next(j):
+        later = 1 - lax.rem(j, 2)
+        active[later] = (
+            jax.nn.gelu(gate_buf[later].astype(jnp.float32), approximate=True)
+            * up_buf[later].astype(jnp.float32)
+        ).astype(jnp.bfloat16)
+
+    def leaf_wide(j, cv):
+        ez, ex, other, mine = place(j)
+        color, s = lax.div(cv, 2), 1 - 2 * lax.rem(cv, 2)
+        sp, sq, p, q = axes_of(color)
+        ep = jnp.where(color == 0, ex, ez)
+        eq = jnp.where(color == 0, ez, ex)
+        u = wrap(s * ep)
+
+        @pl.when(u >= 2)
+        def _():
+            step = jnp.where(u == 2, s, -s)
+            target = y * 16 + wrap(p + step) * sp + q * sq
+            slot_of = jnp.where(u == 2, 0, 16) + eq * 2
+            push_wide(cv, other, target, slot_of + 1)
+            push_wide(cv, mine, target, slot_of)
+
+    def leaf_slim(j, cv):
+        ez, ex, other, _ = place(j)
+        color = lax.div(cv, 2)
+        ep = jnp.where(color == 0, ex, ez)
+        eq = jnp.where(color == 0, ez, ex)
+        push_slim(cv, other, flat(1 - y, z, x), ep * 4 + eq)
+
     def compute(j):
-        ez, ex, other, mine = place(j)
-        slot = lax.rem(j, 2)
-
         @pl.when(j + 2 < BLOCKS // 2)
         def _():
             for copy in loads(j + 2):
@@ -225,50 +272,36 @@
             for copy in loads(j + 1):
                 copy.wait()
 
-        later = 1 - slot
-        active[later] = (
-            jax.nn.gelu(gate_buf[later].astype(jnp.float32), approximate=True)
-            * up_buf[later].astype(jnp.float32)
-        ).astype(jnp.bfloat16)
-        hidden = active[slot]
-        places = [pl.ds(pl.multiple_of(block * rows, rows), rows) for block in (other, mine)]
-
-        def product(begin, width):
-            return (
-                jnp.dot(hidden, lag[:, begin : begin + width], preferred_element_type=jnp.float32) * inv_root
-            ).astype(jnp.bfloat16)
-
+        activate_next(j)
         for color in range(2):
-            value = product(color * wcols, wcols)
-            for i, here in enumerate(places):
-                wide[color, here, :] = value[i * rows : (i + 1) * rows]
+            keep_product(j, wide, color, color * wcols)
         for color in range(2):
-            value = product(2 * wcols + color * scols, scols)
-            for i, here in enumerate(places):
-                slim[color, here, :] = value[i * rows : (i + 1) * rows]
-        for i, here in enumerate(places):
-            hid[:, here] = hidden[i * rows : (i + 1) * rows].T
-
-        def leaf(cv):
-            color, s = lax.div(cv, 2), 1 - 2 * lax.rem(cv, 2)
-            sp, sq, p, q = axes_of(color)
-            ep = jnp.where(color == 0, ex, ez)
-            eq = jnp.where(color == 0, ez, ex)
-            u = wrap(s * ep)
-            push_slim(cv, other, flat(1 - y, z, x), ep * 4 + eq)
-
-            @pl.when(u >= 2)
-            def _():
-                step = jnp.where(u == 2, s, -s)
-                target = y * 16 + wrap(p + step) * sp + q * sq
-                slot_of = jnp.where(u == 2, 0, 16) + eq * 2
-                push_wide(cv, other, target, slot_of + 1)
-                push_wide(cv, mine, target, slot_of)
-
-        each(4, leaf)
-
-    lag_copy.wait()
-    each(BLOCKS // 2, compute)
+            keep_product(j, slim, color, 2 * wcols + color * scols)
+        keep_hidden(j)
+
+        def leaves(cv):
+            leaf_slim(j, cv)
+            leaf_wide(j, cv)
+
+        each(4, leaves)
+
+    for color in range(2):
+        lag_copies[color].wait()
+        keep_product(0, wide, color, color * wcols)
+        if color == 0:
+            meet(plane() + across())
+        each(2, lambda i: leaf_wide(0, 2 * color + i))
+    lag_copies[2].wait()
+    for color in range(2):
+        keep_product(0, slim, color, 2 * wcols + color * scols)
+        each(2, lambda i: leaf_slim(0, 2 * color + i))
+    for copy in loads(2):
+        copy.start()
+    for copy in loads(1):
+        copy.wait()
+    keep_hidden(0)
+    activate_next(0)
+    each(BLOCKS // 2 - 1, lambda j: compute(j + 1))
 
     def gather(total, parts):
         def tile(i):
@@ -609,13 +642,16 @@
     def group(n):
         for i in range(1, len(ORDER) - 1):
             pl.when(n == i)(functools.partial(steps_of, ORDER[i], bodies))
-        for begin, product in parts_of(n):
+        which = GROUPS[0]
+        for i in range(1, len(GROUPS) - 1):
+            which = jnp.where(n == i, GROUPS[i], which)
+        for begin, product in parts_of(which):
             total[:, begin : begin + product.shape[1]] += product
 
     each(7, group)
     steps_of(ORDER[7], bodies)
     kept = (zero, zero, zero)
-    for part, (begin, product) in enumerate(parts_of(7)):
+    for part, (begin, product) in enumerate(parts_of(GROUPS[7])):
         columns = column_parts[part]
         grad[:, columns] = ((total[:, columns] + product) * inv_root).astype(jnp.bfloat16)
         grad_copy(part).start()
@@ -638,21 +674,21 @@
         for copy in copies:
             copy.wait_recv()
 
-    pol = lax.axis_index("pol")
-    exchange(0, (0, 1, 2), [(pol, flat(y, z, wrap(x + i))) for i in (1, 2, 3)])
-    sums[1] = sums[0] + sums_in[0] + sums_in[1] + sums_in[2]
-    exchange(1, (3, 4, 5), [(pol, flat(y, wrap(z + i), x)) for i in (1, 2, 3)])
-    sums[2] = sums[1] + sums_in[3] + sums_in[4] + sums_in[5]
-    exchange(2, (6, 7, 8), [(pol, flat(1 - y, z, x)), (partner(), me), (partner(), flat(1 - y, z, x))])
-    own_sums = jnp.sum(sums[2] + sums_in[6], axis=1, keepdims=True)
-    part_sums = jnp.sum(sums_in[7] + sums_in[8], axis=1, keepdims=True)
+    exchange(0, range(15), plane())
+    partly = sums[0]
+    for i in range(15):
+        partly = partly + sums_in[i]
+    sums[1] = partly
+    exchange(1, (15, 16, 17), across())
+    own_sums = jnp.sum(sums[1] + sums_in[16], axis=1, keepdims=True)
+    part_sums = jnp.sum(sums_in[15] + sums_in[17], axis=1, keepdims=True)
 
     def spread_row(column, i):
         return jnp.broadcast_to(column[i : i + 1], (1, 128))
 
     grad_oo, tgrad_oo, tgrad_po, task_oo, task_op, grad_op = (spread_row(own_sums, i) for i in range(6))
     grad_pp, tgrad_pp, tgrad_op, task_pp = (spread_row(part_sums, i) for i in range(4))
-    is_first = lax.rem(pol, 2) == 0
+    is_first = lax.rem(lax.axis_index("pol"), 2) == 0
     scale_own = step_rate * clip_factor(grad_oo)
     scale_part = step_rate * clip_factor(grad_pp)
     own_total = task_oo - 2.0 * scale_own * tgrad_oo + scale_own * scale_own * grad_oo
@@ -725,9 +761,10 @@
             pltpu.VMEM((ff, cols), jnp.float32),
             *[pltpu.VMEM((ff, cols), bf16)] * 3,
             pltpu.VMEM((rows, 128), jnp.float32),
-            pltpu.VMEM((3, 8, 128), jnp.float32),
-            pltpu.VMEM((9, 8, 128), jnp.float32),
+            pltpu.VMEM((2, 8, 128), jnp.float32),
+            pltpu.VMEM((18, 8, 128), jnp.float32),
             dma((2, 4)),
+            dma((3,)),
             dma,
             dma,
             dma,
@@ -735,7 +772,7 @@
             dma((4,)),
             dma((2,)),
             dma,
-            dma((9,)),
+            dma((18,)),
             *per_stream,
             *per_stream,
             pltpu.SemaphoreType.REGULAR((2,)),

time: 206 us -> 202 us (0.981)
  Pallas kernels: 199 us -> 196 us
    pallas_call x1, Pallas kernels: 199 us -> 196 us  [shards(): pl.pallas_call(step_kernel, name='policy_step', out_shape=(jax.ShapeDtype...]
where the time goes in v5:
time: 202 us
  Pallas kernels  196 us (97%)
  local copies, waits for them, and re-layouts  5.38 us (3%)
    pallas_call x1, Pallas kernels, shards(): pl.pallas_call(step_kernel, name='policy_step', out_shape=(jax.ShapeDtype...  196 us
    unnamed x4, local copies, waits for them, and re-layouts  5.38 us

profile of v5, /device:TPU:1, one launch (start us, length us, event | category | flops | bytes accessed | tf_op | source)
XLA Modules:
  0.0 201.9 jit_solution(2828570800135888782)
XLA Ops:
  0.6 195.9 %policy_step.1 = (bf16[640,2304]{1,0:T(8,128)(2,1)}, bf16[640,2304]{1,0:T(8,128)(2,1)}) custom-call(bf16[4096,640]{1,0:T(8,128)(2,1)} %bitcast.9, bf16[4096,640]{1,0:T(8,128)(2,1)} %bitcast.10, bf16[640,2304]{1,0:T(8,128)(2,1)} %bitcast.11, bf16[640,2304]{1,0:T(8,128)(2,1)} %bitcast.12, bf16[128,2304]{1,0:T(8,128)(2,1)} %bitcast.13, s32[1,128]{1,0:T(1,128)} %buckets.1, ...), custom_call_target="tpu_custom_call" | custom-call | flops 24159191040 | bytes 15728640 | tf_op jit(solution)/shard_map/policy_step/pallas_call | solution.py:747
  196.5 0.0 copy-start
  196.5 3.8 %copy.11 = bf16[1,640,2304]{2,1,0:T(8,128)(2,1)} copy(bf16[1,640,2304]{2,1,0:T(8,128)(2,1)} %bitcast.8) | data formatting | bytes 5898240
  200.3 0.0 copy-done
  200.3 1.6 copy.12
Async XLA Ops:
  196.5 3.8 %copy-start = (bf16[640,2304]{1,0:T(8,128)(2,1)S(1)}, bf16[640,2304]{1,0:T(8,128)(2,1)}, u32[]{:S(2)}) copy-start(bf16[640,2304]{1,0:T(8,128)(2,1)} %get-tuple-element.5) | copy-start | bytes 8847364

commit v6 on v5

--- a/solution.py
+++ b/solution.py
@@ -17,7 +17,7 @@
 ema_rate = 0.1
 
 MESH = pl.DeviceIdType.MESH
-VMEM_BYTES = 67_000_000
+VMEM_BYTES = 60_600_000
 RING = 4
 BLOCKS = 32
 
@@ -151,10 +151,10 @@
 
 def step_kernel(
     gate, up, lag_in, task_in, cot, buckets, adv,
-    lag_out, merged_out,
-    gate_buf, up_buf, active, lag, hid, wide, slim, wide_in, slim_in,
-    total, other_task, grad, other_grad, scale, sums, sums_in,
-    load_sem, lag_sem, task_sem, task_send, task_recv, grad_send, grad_recv, out_sem, sums_send, sums_recv,
+    lag, other_grad,
+    gate_buf, up_buf, active, hid, wide, slim, wide_in, slim_in,
+    total, other_task, grad, scale, sums, sums_in,
+    load_sem, lag_sem, task_sem, task_send, task_recv, grad_send, grad_recv, sums_send, sums_recv,
     fold_wide_send, fold_slim_send, fold_wide_recv, fold_slim_recv,
     wide_send, slim_send, wide_recv, slim_recv, clear,
 ):
@@ -719,12 +719,6 @@
                 other_grad[at, lanes] = (weight_own * delta_own + weight_part * delta_part).astype(jnp.bfloat16)
 
         each(band // tile, lambda k: settle_outputs(i * (band // tile) + k))
-        at = pl.ds(i * band, band)
-        pltpu.make_async_copy(lag.at[at], lag_out.at[at], out_sem.at[0]).start()
-        pltpu.make_async_copy(other_grad.at[at], merged_out.at[at], out_sem.at[1]).start()
-
-    pltpu.make_async_copy(lag, lag_out, out_sem.at[0]).wait()
-    pltpu.make_async_copy(other_grad, merged_out, out_sem.at[1]).wait()
     task_swap.wait_send()
     remote_to(grad, other_grad, grad_send, grad_recv.at[0], (partner(), me)).wait_send()
     remote_to(sums_in, sums_in, sums_send, sums_recv.at[0], (partner(), me)).wait_send()
@@ -747,19 +741,18 @@
     new_lag, merged = pl.pallas_call(
         step_kernel,
         name="policy_step",
-        out_shape=(jax.ShapeDtypeStruct((ff, cols), bf16), jax.ShapeDtypeStruct((ff, cols), bf16)),
+        out_shape=(pltpu.VMEM((ff, cols), bf16), pltpu.VMEM((ff, cols), bf16)),
         in_specs=[any_spec] * 4 + [vmem_spec] * 3,
-        out_specs=(any_spec, any_spec),
+        out_specs=(vmem_spec, vmem_spec),
         scratch_shapes=[
             *[pltpu.VMEM((2, 2 * rows, ff), bf16)] * 3,
-            pltpu.VMEM((ff, cols), bf16),
             pltpu.VMEM((ff, tokens), bf16),
             pltpu.VMEM((2, tokens, wcols), bf16),
             pltpu.VMEM((2, tokens, scols), bf16),
             pltpu.VMEM((4, BLOCKS - 1, half, wcols), bf16),
             pltpu.VMEM((4, BLOCKS - 1, half, scols), bf16),
             pltpu.VMEM((ff, cols), jnp.float32),
-            *[pltpu.VMEM((ff, cols), bf16)] * 3,
+            *[pltpu.VMEM((ff, cols), bf16)] * 2,
             pltpu.VMEM((rows, 128), jnp.float32),
             pltpu.VMEM((2, 8, 128), jnp.float32),
             pltpu.VMEM((18, 8, 128), jnp.float32),
@@ -770,7 +763,6 @@
             dma,
             dma,
             dma((4,)),
-            dma((2,)),
             dma,
             dma((18,)),
             *per_stream,

time: 202 us -> 199 us (0.985)
  local copies, waits for them, and re-layouts: 5.38 us -> 3.2 us
    unnamed x4 -> x2, local copies, waits for them, and re-layouts: 5.38 us -> 3.2 us
where the time goes in v6:
time: 199 us
  Pallas kernels  195 us (98%)
  local copies, waits for them, and re-layouts  3.2 us (2%)
    pallas_call x1, Pallas kernels, shards(): pl.pallas_call(step_kernel, name='policy_step', out_shape=(pltpu.VMEM((ff...  195 us

profile of v6, /device:TPU:1, one launch (start us, length us, event | category | flops | bytes accessed | tf_op | source)
XLA Modules:
  0.0 198.9 jit_solution(15144236649934961874)
XLA Ops:
  0.6 195.0 %policy_step.1 = (bf16[640,2304]{1,0:T(8,128)(2,1)S(1)}, bf16[640,2304]{1,0:T(8,128)(2,1)S(1)}) custom-call(bf16[4096,640]{1,0:T(8,128)(2,1)} %bitcast.9, bf16[4096,640]{1,0:T(8,128)(2,1)} %bitcast.10, bf16[640,2304]{1,0:T(8,128)(2,1)} %bitcast.11, bf16[640,2304]{1,0:T(8,128)(2,1)} %bitcast.12, bf16[128,2304]{1,0:T(8,128)(2,1)} %bitcast.13, ...), custom_call_target="tpu_custom_call" | custom-call | flops 24159191040 | bytes 15728640 | tf_op jit(solution)/shard_map/policy_step/pallas_call | solution.py:741
  195.7 1.6 copy.11
  197.3 1.6 copy.12
